TPU v7x, 256 devices: a whole 4x4x8 slice. The times are simulated.
256 devices in a mesh: pair: 64 (over y, z, x_lo), sec: 4 (over x_hi, core).
Axes of the slice: x: 4 (x_hi: 2, x_lo: 2; x = x_hi * 2 + x_lo), y: 4, z: 8, core: 2. Of those that a mesh axis runs over, the one named last changes fastest.
Arguments:
- psi: bfloat16 [32, 768, 384], P('sec'), may hold values from -6 to 6
- sec_rows: int32 [32], replicated, may hold values from 128 to 768, as said below
- match: int32 [32], replicated, may hold values from 0 to 31, each once
- normal_ops: bfloat16 [64, 32, 768, 768], P('pair', 'sec'), may hold values from -0.02734375 to 0.02734375
- comp_ops: bfloat16 [64, 32, 384, 384], P('pair', 'sec'), may hold values from -0.3125 to 0.3125
Outputs:
- sigma: bfloat16 [32, 768, 384], P('sec', 'pair')
Inputs may be any that keep to these rules, and one draw needn't show every extreme that they name: `sec_rows`: every entry is a multiple of 128; some entry equals 768 in every draw.
All inputs are finite; a program needn't handle non-finite values.
Results may differ from a plain program's by a relative error of at most 0.0049.
Values may be sent and summed in bfloat16 or wider, within the bound.
No kernel may reach another device: no remote copies, remote signals or barrier semaphores. Data moves between devices by JAX's collectives and lax.ppermute only.
A program may use at most 128 MiB of HBM per device.

v0:
```python
import jax
import jax.numpy as jnp
from jax import lax
from jax.sharding import PartitionSpec as P


def from_partner(value, axis, distance):
    mask = 2**distance
    pairs = [(source, source ^ mask) for source in range(lax.axis_size(axis))]
    return lax.ppermute(value, axis, pairs)


def pick_sources(gathered, match, targets):
    total = match.shape[0]
    hits = match[None, :] == targets[:, None]
    source = jnp.sum(jnp.where(hits, jnp.arange(total, dtype=jnp.int32)[None, :], 0), axis=1)
    return gathered[source]


def shards(psi, sec_rows, match, normal_ops, comp_ops):
    sec_dev = psi.shape[0]
    block_rows = psi.shape[1]
    first = lax.axis_index("sec") * sec_dev
    targets = first + jnp.arange(sec_dev, dtype=jnp.int32)
    rows_here = lax.dynamic_slice_in_dim(sec_rows, first, sec_dev)
    line = jnp.arange(block_rows, dtype=jnp.int32)
    kept = jnp.where((line[None, :] < rows_here[:, None])[:, :, None], psi, jnp.zeros_like(psi))
    levels = lax.axis_size("pair").bit_length() - 1
    mirrored = comp_ops
    for bit in range(levels):
        mirrored = from_partner(mirrored, "pair", bit)
    mirrored = mirrored[::-1]
    half = jnp.einsum(
        "psab,sbc->psac", normal_ops, kept, preferred_element_type=jnp.float32
    ).astype(jnp.bfloat16)
    terms = jnp.einsum("psac,psdc->sad", half, mirrored, preferred_element_type=jnp.float32)
    share = block_rows // lax.axis_size("pair")
    row_start = lax.axis_index("pair") * share
    partial_rows = lax.psum_scatter(terms, "pair", scatter_dimension=1, tiled=True).astype(
        jnp.bfloat16
    )
    gathered = lax.all_gather(partial_rows, "sec", axis=0, tiled=True)
    summed = pick_sources(gathered, match, targets)
    target_rows = lax.dynamic_slice_in_dim(sec_rows, first, sec_dev)
    my_lines = row_start + jnp.arange(share, dtype=jnp.int32)
    out_keep = my_lines[None, :] < target_rows[:, None]
    return jnp.where(out_keep[:, :, None], summed, jnp.zeros_like(summed))


def solution(mesh):
    in_specs = (
        P("sec", None, None),
        P(),
        P(),
        P("pair", "sec", None, None),
        P("pair", "sec", None, None),
    )
    out_specs = P("sec", "pair", None)
    return jax.shard_map(shards, mesh=mesh, in_specs=in_specs, out_specs=out_specs, check_vma=False)
```

profile of v0, /device:TPU:1, one launch (start us, length us, event | category | flops | bytes accessed | tf_op | source)
XLA Modules:
  0.0 812.5 jit_solution(509405714150790284)
XLA Ops:
  6.5 0.0 reduce-scatter.2.cloned.1.call-start
  6.5 2.0 collective-permute-start
  8.6 50.0 %collective-permute-done = bf16[1,8,384,384]{3,2,1,0:T(8,128)(2,1)S(1)} collective-permute-done((bf16[1,8,384,384]{3,2,1,0:T(8,128)(2,1)}, bf16[1,8,384,384]{3,2,1,0:T(8,128)(2,1)S(1)}, u32[]{:S(2)}, u32[]{:S(2)}) %collective-permute-start) | collective-permute-done | bytes 2359328 | tf_op jit(solution)/shard_map/ppermute | solution.py:10
  58.6 2.7 collective-permute-start.1
  61.3 50.1 %collective-permute-done.1 = bf16[1,8,384,384]{3,2,1,0:T(8,128)(2,1)S(1)} collective-permute-done((bf16[1,8,384,384]{3,2,1,0:T(8,128)(2,1)S(1)}, bf16[1,8,384,384]{3,2,1,0:T(8,128)(2,1)S(1)}, u32[]{:S(2)}, u32[]{:S(2)}) %collective-permute-start.1) | collective-permute-done | bytes 2359328 | tf_op jit(solution)/shard_map/ppermute | solution.py:10
  111.4 2.9 collective-permute-start.2
  114.3 101.3 %collective-permute-done.2 = bf16[1,8,384,384]{3,2,1,0:T(8,128)(2,1)S(1)} collective-permute-done((bf16[1,8,384,384]{3,2,1,0:T(8,128)(2,1)S(1)}, bf16[1,8,384,384]{3,2,1,0:T(8,128)(2,1)S(1)}, u32[]{:S(2)}, u32[]{:S(2)}) %collective-permute-start.2) | collective-permute-done | bytes 2359328 | tf_op jit(solution)/shard_map/ppermute | solution.py:10
  215.6 6.5 collective-permute-start.3
  222.1 101.8 %collective-permute-done.3 = bf16[1,8,384,384]{3,2,1,0:T(8,128)(2,1)S(1)} collective-permute-done((bf16[1,8,384,384]{3,2,1,0:T(8,128)(2,1)S(1)}, bf16[1,8,384,384]{3,2,1,0:T(8,128)(2,1)S(1)}, u32[]{:S(2)}, u32[]{:S(2)}) %collective-permute-start.3) | collective-permute-done | bytes 2359328 | tf_op jit(solution)/shard_map/ppermute | solution.py:10
  323.9 1.3 collective-permute-start.4
  325.2 49.9 %collective-permute-done.4 = bf16[1,8,384,384]{3,2,1,0:T(8,128)(2,1)S(1)} collective-permute-done((bf16[1,8,384,384]{3,2,1,0:T(8,128)(2,1)S(1)}, bf16[1,8,384,384]{3,2,1,0:T(8,128)(2,1)S(1)}, u32[]{:S(2)}, u32[]{:S(2)}) %collective-permute-start.4) | collective-permute-done | bytes 2359328 | tf_op jit(solution)/shard_map/ppermute | solution.py:10
  375.1 2.9 collective-permute-start.5
  378.0 0.7 dynamic_slice.4
  378.7 0.1 iota_compare_fusion
  378.8 48.8 %collective-permute-done.5 = bf16[1,8,384,384]{3,2,1,0:T(8,128)(2,1)} collective-permute-done((bf16[1,8,384,384]{3,2,1,0:T(8,128)(2,1)S(1)}, bf16[1,8,384,384]{3,2,1,0:T(8,128)(2,1)}, u32[]{:S(2)}, u32[]{:S(2)}) %collective-permute-start.5) | collective-permute-done | bytes 2359328 | tf_op jit(solution)/shard_map/ppermute | solution.py:10
  427.6 13.8 %fusion.2 = f32[8,768,384]{2,1,0:T(8,128)} fusion(bf16[1,8,768,768]{3,2,1,0:T(8,128)(2,1)} %param.8, bf16[8,768,384]{2,1,0:T(8,128)(2,1)} %param.5, pred[8,768]{1,0:T(8,128)(4,1)S(1)} %iota_compare_fusion, bf16[1,8,384,384]{3,2,1,0:T(8,128)(2,1)} %collective-permute-done.5), kind=kOutput, calls=%fused_computation.3 | convolution fusion | flops 5440536576 | bytes 25958400 | tf_op jit(solution)/shard_map/psac,psdc->sad/dot_general | solution.py:36
  441.4 12.8 %copy.19 = f32[8,768,384]{2,0,1:T(8,128)} copy(f32[8,768,384]{2,1,0:T(8,128)} %fusion.2) | data formatting | bytes 18874368 | tf_op jit(solution)/shard_map/psac,psdc->sad/dot_general | solution.py:36
  454.2 0.0 copy-start
  454.2 0.0 reduce-scatter.2.cloned.1.call-update
  454.3 0.6 copy-done
  454.9 0.2 select_reduce_fusion
  455.1 0.1 broadcast_compare_fusion
  455.1 293.0 %reduce-scatter.2.cloned.1.call-done = f32[8,12,384]{2,0,1:T(8,128)} async-done(((f32[8,768,384]{2,0,1:T(8,128)}), f32[8,12,384]{2,0,1:T(8,128)}) %reduce-scatter.2.cloned.1.call-update) | async-done | bytes 147472 | tf_op jit(solution)/shard_map/reduce_scatter | solution.py:39
  748.2 0.9 convert_element_type.15
  749.1 55.1 %all_gather.3 = bf16[32,12,384]{2,0,1:T(8,128)(2,1)S(1)} all-gather(bf16[8,12,384]{2,0,1:T(8,128)(2,1)S(1)} %convert_element_type.15), channel_id=1, replica_groups=mesh['pair'=64,'sec'=4] {'sec'}, dimensions={0}, use_global_device_ids=true | all-gather | bytes 368640 | tf_op jit(solution)/shard_map/all_gather | solution.py:42
  804.2 0.1 copy.20
  804.3 0.6 gather_fusion
  804.9 0.1 broadcast_select_fusion
  805.0 0.6 copy.21
  (4 shorter events, 0.0 us)
Async XLA Ops:
  6.5 741.6 %reduce-scatter.2.cloned.1.call-start = ((), (), s32[]{:S(2)}) async-start(), calls=%async_computation.1 | async-start | bytes 9584640 | tf_op jit(solution)/shard_map/reduce_scatter | solution.py:39
  6.5 52.1 %collective-permute-start = (bf16[1,8,384,384]{3,2,1,0:T(8,128)(2,1)}, bf16[1,8,384,384]{3,2,1,0:T(8,128)(2,1)S(1)}, u32[]{:S(2)}, u32[]{:S(2)}) collective-permute-start(bf16[1,8,384,384]{3,2,1,0:T(8,128)(2,1)} %param.9), channel_id=1, source_target_pairs={{0,4},{4,0},{8,12},{12,8},{16,20},{20,16},{24,28},{28,24},{32,36},... | collective-permute-start | bytes 7077896 | tf_op jit(solution)/shard_map/ppermute | solution.py:10
  58.6 52.8 %collective-permute-start.1 = (bf16[1,8,384,384]{3,2,1,0:T(8,128)(2,1)S(1)}, bf16[1,8,384,384]{3,2,1,0:T(8,128)(2,1)S(1)}, u32[]{:S(2)}, u32[]{:S(2)}) collective-permute-start(bf16[1,8,384,384]{3,2,1,0:T(8,128)(2,1)S(1)} %collective-permute-done), channel_id=1, source_target_pairs={{0,8},{4,12},{8,0},{12,4},{16,24},{20,28},{24,16},{28,20},{32,40},... | collective-permute-start | bytes 7077896 | tf_op jit(solution)/shard_map/ppermute | solution.py:10
  111.4 104.1 %collective-permute-start.2 = (bf16[1,8,384,384]{3,2,1,0:T(8,128)(2,1)S(1)}, bf16[1,8,384,384]{3,2,1,0:T(8,128)(2,1)S(1)}, u32[]{:S(2)}, u32[]{:S(2)}) collective-permute-start(bf16[1,8,384,384]{3,2,1,0:T(8,128)(2,1)S(1)} %collective-permute-done.1), channel_id=1, source_target_pairs={{0,16},{4,20},{8,24},{12,28},{16,0},{20,4},{24,8},{28,12},{32,48},... | collective-permute-start | bytes 7077896 | tf_op jit(solution)/shard_map/ppermute | solution.py:10
  215.6 108.3 %collective-permute-start.3 = (bf16[1,8,384,384]{3,2,1,0:T(8,128)(2,1)S(1)}, bf16[1,8,384,384]{3,2,1,0:T(8,128)(2,1)S(1)}, u32[]{:S(2)}, u32[]{:S(2)}) collective-permute-start(bf16[1,8,384,384]{3,2,1,0:T(8,128)(2,1)S(1)} %collective-permute-done.2), channel_id=1, source_target_pairs={{0,32},{4,36},{8,40},{12,44},{16,48},{20,52},{24,56},{28,60},{32,0... | collective-permute-start | bytes 7077896 | tf_op jit(solution)/shard_map/ppermute | solution.py:10
  323.9 51.2 %collective-permute-start.4 = (bf16[1,8,384,384]{3,2,1,0:T(8,128)(2,1)S(1)}, bf16[1,8,384,384]{3,2,1,0:T(8,128)(2,1)S(1)}, u32[]{:S(2)}, u32[]{:S(2)}) collective-permute-start(bf16[1,8,384,384]{3,2,1,0:T(8,128)(2,1)S(1)} %collective-permute-done.3), channel_id=1, source_target_pairs={{0,64},{4,68},{8,72},{12,76},{16,80},{20,84},{24,88},{28,92},{32,9... | collective-permute-start | bytes 7077896 | tf_op jit(solution)/shard_map/ppermute | solution.py:10
  375.1 52.5 %collective-permute-start.5 = (bf16[1,8,384,384]{3,2,1,0:T(8,128)(2,1)S(1)}, bf16[1,8,384,384]{3,2,1,0:T(8,128)(2,1)}, u32[]{:S(2)}, u32[]{:S(2)}) collective-permute-start(bf16[1,8,384,384]{3,2,1,0:T(8,128)(2,1)S(1)} %collective-permute-done.4), channel_id=1, source_target_pairs={{0,128},{4,132},{8,136},{12,140},{16,144},{20,148},{24,152},{28,15... | collective-permute-start | bytes 7077896 | tf_op jit(solution)/shard_map/ppermute | solution.py:10
  454.2 0.7 copy-start
Sparse Core Ops, SparseCore 0:
  454.4 293.7 reduce-scatter.1
where the time goes:
time: 813 us; the launch traced here: 812 us
  waiting for transfers between devices  695 us (85%)
  blocking collectives  55.1 us (7%)
  starting transfers between devices  18.3 us (2%)
  local copies, waits for them, and re-layouts  15.4 us (2%)
  matrix products  13.8 us (2%)
  between operations  13.4 us (2%)
    ppermute x6, waiting for transfers between devices, from_partner(): return lax.ppermute(value, axis, pairs)  402 us
    reduce_scatter x1, waiting for transfers between devices, shards(): lax.psum_scatter(terms, 'pair', scatter_dimension=1, tiled=True)  293 us
    all_gather x1, blocking collectives, shards(): gathered = lax.all_gather(partial_rows, 'sec', axis=0, tiled=True)  55.1 us
    ppermute x6, starting transfers between devices, from_partner(): return lax.ppermute(value, axis, pairs)  18.3 us
  transfers between devices with their start and end apart: 7, of which 7 were waited for; matrix products, arithmetic and copies ran while one was open for 0% of the time, Pallas kernels for 0%

commit v1 on v0

v1 whole, which is shorter than its diff:
```python
import jax
import jax.numpy as jnp
from jax import lax
from jax.experimental import pallas as pl
from jax.sharding import PartitionSpec as P


INTERPRET = False
YS, ZS, XS = 4, 8, 2
CHUNKS = ((0, 1), (1, 2), (2, 4), (4, 6), (6, 7), (7, 8))
GROUPS = ((0, 1), (2, 3, 4, 5))
SWAPPED = (4,)
F32, BF16 = jnp.float32, jnp.bfloat16


def split_pair(p):
    return p // (ZS * XS), (p // XS) % ZS, p % XS


def join_pair(y, z, x):
    return (y * ZS + z) * XS + x


def perm_of(move):
    return [(p, join_pair(*move(*split_pair(p)))) for p in range(YS * ZS * XS)]


MIRROR = perm_of(lambda y, z, x: (YS - 1 - y, ZS - 1 - z, XS - 1 - x))
STAGES = {
    "a": perm_of(lambda y, z, x: (y ^ 1, z, x)),
    "b": perm_of(lambda y, z, x: (y, z ^ 1, x)),
}


FOURS = {
    "c": (
        perm_of(lambda y, z, x: (y, z, x ^ 1)),
        perm_of(lambda y, z, x: (YS - 1 - y, z, x)),
        perm_of(lambda y, z, x: (YS - 1 - y, z, x ^ 1)),
    ),
    "e": (
        perm_of(lambda y, z, x: (y, z ^ 2, x)),
        perm_of(lambda y, z, x: (y, z ^ 4, x)),
        perm_of(lambda y, z, x: (y, z ^ 6, x)),
    ),
}


def routed_rows(pair, line, share, swapped):
    y, z, x = split_pair(pair)
    a, b, c, e = [(line // (share * n)) % m for n, m in ((32, 2), (16, 2), (4, 4), (1, 4))]
    if swapped:
        a, b = b, a
    near = y ^ a
    owner_y = jnp.where(c >= 2, YS - 1 - near, near)
    return share * join_pair(owner_y, z ^ (b + 2 * e), x ^ (c % 2)) + line % share


def pick_sources(gathered, match, targets):
    total = match.shape[0]
    hits = match[None, :] == targets[:, None]
    source = jnp.sum(jnp.where(hits, jnp.arange(total, dtype=jnp.int32)[None, :], 0), axis=1)
    return gathered[source]


def terms_kernel(half_ref, comp_ref, keep_ref, send_ref):
    rows = keep_ref.shape[1]
    for part, ref in ((1, send_ref), (0, keep_ref)):
        ref[0] = lax.dot_general(
            half_ref[0, part * rows : (part + 1) * rows],
            comp_ref[0],
            (((1,), (1,)), ((), ())),
            preferred_element_type=F32,
        ).astype(ref.dtype)


def terms_of(half, comp, start):
    sectors, cols, _ = comp.shape
    rows = half.shape[1]
    spec = pl.BlockSpec((1, rows // 2, cols), lambda s: (s, 0, 0))
    return pl.pallas_call(
        terms_kernel,
        grid=(sectors,),
        in_specs=[
            pl.BlockSpec((1, rows, cols), lambda s: (s + start, 0, 0)),
            pl.BlockSpec((1, cols, cols), lambda s: (s, 0, 0)),
        ],
        out_specs=[spec, spec],
        out_shape=[
            jax.ShapeDtypeStruct((sectors, rows // 2, cols), F32),
            jax.ShapeDtypeStruct((sectors, rows // 2, cols), BF16),
        ],
        interpret=INTERPRET,
        name="terms",
    )(half, comp)


def exchange(value, perm):
    return lax.ppermute(value, "pair", perm)


def fold(total, got):
    total = total + got.astype(F32)
    cut = total.shape[1] // 2
    return total[:, :cut], total[:, cut:].astype(BF16)


def product(psi, sec_rows, match, normal_ops, comp_ops):
    sec_dev, block_rows, _ = psi.shape
    pairs = lax.axis_size("pair")
    share = block_rows // pairs
    first_sec = lax.axis_index("sec") * sec_dev
    pair = lax.axis_index("pair")
    targets = first_sec + jnp.arange(sec_dev, dtype=jnp.int32)
    rows_here = lax.dynamic_slice_in_dim(sec_rows, first_sec, sec_dev)

    mirrored = [exchange(comp_ops[0, a:b], MIRROR) for a, b in CHUNKS]

    line = jnp.arange(block_rows, dtype=jnp.int32)
    kept = jnp.where((line[None, :] < rows_here[:, None])[:, :, None], psi, jnp.zeros_like(psi))
    half = jnp.einsum("sab,sbc->sac", normal_ops[0], kept, preferred_element_type=F32).astype(BF16)
    routed = []
    for swapped in (False, True):
        rows = routed_rows(pair, line, share, swapped)
        order = (rows[:, None] == line[None, :]).astype(BF16)
        first, end = (CHUNKS[SWAPPED[0]][0], CHUNKS[SWAPPED[-1]][1]) if swapped else (0, sec_dev)
        part = jnp.einsum("ia,sac->sic", order, half[first:end], preferred_element_type=F32)
        routed.append((part.astype(BF16), first))

    flows = []
    for i, (a, _) in enumerate(CHUNKS):
        comp = mirrored[i]
        if i:
            comp, _ = lax.optimization_barrier((comp, flows[-1][1]))
        source, start = routed[i in SWAPPED]
        flows.append(terms_of(source, comp, a - start))
    pieces = []
    for group in GROUPS:
        parts = []
        for i in group:
            keep, send = flows[i]
            near, far = "ba" if i in SWAPPED else "ab"
            got = exchange(send, STAGES[near])
            keep, send = fold(keep, got)
            got = exchange(send, STAGES[far])
            parts.append(keep + got.astype(F32))
        total = jnp.concatenate(parts, axis=0)
        for stage in "ce":
            cut = total.shape[1] // 4
            got = [
                exchange(total[:, (n + 1) * cut : (n + 2) * cut].astype(BF16), FOURS[stage][n])
                for n in range(3)
            ]
            total = total[:, :cut] + sum(value.astype(F32) for value in got)
        pieces.append(total.astype(BF16))

    partial_rows = jnp.concatenate(pieces, axis=0)
    gathered = lax.all_gather(partial_rows, "sec", axis=0, tiled=True)
    summed = pick_sources(gathered, match, targets)
    my_lines = pair * share + jnp.arange(share, dtype=jnp.int32)
    out_keep = my_lines[None, :] < rows_here[:, None]
    return jnp.where(out_keep[:, :, None], summed, jnp.zeros_like(summed))


def solution(mesh):
    in_specs = (
        P("sec", None, None),
        P(),
        P(),
        P("pair", "sec", None, None),
        P("pair", "sec", None, None),
    )
    out_specs = P("sec", "pair", None)
    return jax.shard_map(product, mesh=mesh, in_specs=in_specs, out_specs=out_specs, check_vma=False)
```

time: 813 us -> 216 us (0.27)
  waiting for transfers between devices: 695 us -> 106 us
  blocking collectives: 55.1 us -> 16 us
  starting transfers between devices: 18.3 us -> 53.4 us
  Pallas kernels: 0 us -> 16.3 us
  between operations: 13.4 us -> 0.48 us
  local copies, waits for them, and re-layouts: 15.4 us -> 5.69 us
    ppermute x6 -> x30, waiting for transfers between devices: 402 us -> 106 us  [exchange(): return lax.ppermute(value, 'pair', perm)]
    reduce_scatter x1 -> x0, waiting for transfers between devices: 293 us -> none  [shards(): lax.psum_scatter(terms, 'pair', scatter_dimension=1, tiled=True)]
    all_gather x1, blocking collectives: 55.1 us -> 16 us  [product(): gathered = lax.all_gather(partial_rows, 'sec', axis=0, tiled=True)]
    ppermute x6 -> x30, starting transfers between devices: 18.3 us -> 53.4 us  [exchange(): return lax.ppermute(value, 'pair', perm)]
    pallas_call x0 -> x6, Pallas kernels: none -> 16.3 us  [terms_of(): pl.pallas_call(terms_kernel, grid=(sectors,), in_specs=[pl.BlockSpec((1,...]
    dot_general x1 -> x0, local copies, waits for them, and re-layouts: 12.8 us -> none  [shards(): jnp.einsum('psac,psdc->sad', half, mirrored, preferred_element_type=jnp.f...]
    dot_general x1 -> x3, matrix products: 13.8 us -> 16.9 us  [the longest x2 8.47 us: product(): jnp.einsum('ia,sac->sic', order, half[first:end], preferred_element_type=...]
  transfers between devices with their start and end apart: 7 -> 30, of which waited for: 7 -> 12; matrix products, arithmetic and copies ran while one was open for 0% -> 9% of each run, Pallas kernels for 0% -> 8%
where the time goes in v1:
time: 216 us
  waiting for transfers between devices  106 us (49%)
  starting transfers between devices  53.4 us (25%)
  matrix products  16.9 us (8%)
  Pallas kernels  16.3 us (8%)
  blocking collectives  16 us (7%)
  local copies, waits for them, and re-layouts  5.69 us (3%)
    ppermute x30, waiting for transfers between devices, exchange(): return lax.ppermute(value, 'pair', perm)  106 us
    ppermute x30, starting transfers between devices, exchange(): return lax.ppermute(value, 'pair', perm)  53.4 us
    pallas_call x6, Pallas kernels, terms_of(): pl.pallas_call(terms_kernel, grid=(sectors,), in_specs=[pl.BlockSpec((1,...  16.3 us
    all_gather x1, blocking collectives, product(): gathered = lax.all_gather(partial_rows, 'sec', axis=0, tiled=True)  16 us
    dot_general x2, matrix products, product(): jnp.einsum('ia,sac->sic', order, half[first:end], preferred_element_type=...  8.47 us
    dot_general x1, matrix products, product(): jnp.einsum('sab,sbc->sac', normal_ops[0], kept, preferred_element_type=F32)  8.39 us
  transfers between devices with their start and end apart: 30, of which 12 were waited for; matrix products, arithmetic and copies ran while one was open for 9% of the time, Pallas kernels for 8%

profile of v1, /device:TPU:1, one launch (start us, length us, event | category | flops | bytes accessed | tf_op | source)
XLA Modules:
  0.0 216.1 jit_solution(2026674812805132399)
XLA Ops:
  0.0 2.2 %slice_bitcast_fusion.7 = (bf16[1,384,384]{2,1,0:T(8,128)(2,1)}, bf16[1,384,384]{2,1,0:T(8,128)(2,1)S(1)}, bf16[1,384,384]{2,1,0:T(8,128)(2,1)S(1)}, bf16[1,384,384]{2,1,0:T(8,128)(2,1)S(1)}) fusion(bf16[1,8,384,384]{3,2,1,0:T(8,128)(2,1)} %param.9), kind=kLoop, calls=%fused_computation.46 | loop fusion | bytes 2359296 | tf_op jit(solution)/shard_map/squeeze | solution.py:117
  2.2 9.8 %collective-permute-start.21 = (bf16[1,384,384]{2,1,0:T(8,128)(2,1)S(1)}, bf16[1,384,384]{2,1,0:T(8,128)(2,1)S(1)}, u32[]{:S(2)}, u32[]{:S(2)}) collective-permute-start(bf16[1,384,384]{2,1,0:T(8,128)(2,1)S(1)} %get-tuple-element.45), channel_id=1, source_target_pairs={{0,252},{4,248},{8,244},{12,240},{16,236},{20,232},{24,228},{28,22... | collective-permute-start | bytes 884744 | tf_op jit(solution)/shard_map/ppermute | solution.py:99
  12.0 0.1 slice_bitcast_fusion.3
  12.1 0.1 collective-permute-start.15
  12.2 5.7 %collective-permute-start.12 = (bf16[2,384,384]{2,1,0:T(8,128)(2,1)S(1)}, bf16[2,384,384]{2,1,0:T(8,128)(2,1)S(1)}, u32[]{:S(2)}, u32[]{:S(2)}) collective-permute-start(bf16[2,384,384]{2,1,0:T(8,128)(2,1)S(1)} %get-tuple-element.47), channel_id=1, source_target_pairs={{0,252},{4,248},{8,244},{12,240},{16,236},{20,232},{24,228},{28,22... | collective-permute-start | bytes 1769480 | tf_op jit(solution)/shard_map/ppermute | solution.py:99
  17.9 0.1 collective-permute-start.3
  18.0 5.6 %collective-permute-start = (bf16[1,384,384]{2,1,0:T(8,128)(2,1)}, bf16[1,384,384]{2,1,0:T(8,128)(2,1)}, u32[]{:S(2)}, u32[]{:S(2)}) collective-permute-start(bf16[1,384,384]{2,1,0:T(8,128)(2,1)} %get-tuple-element.43), channel_id=1, source_target_pairs={{0,252},{4,248},{8,244},{12,240},{16,236},{20,232},{24,228},{28,22... | collective-permute-start | bytes 884744 | tf_op jit(solution)/shard_map/ppermute | solution.py:99
  23.7 0.1 iota_compare_fusion.7
  23.7 8.4 %convert_bitcast_fusion.1 = bf16[8,768,384]{1,2,0:T(8,128)(2,1)S(1)} fusion(bf16[1,8,768,768]{3,2,1,0:T(8,128)(2,1)} %param.8, bf16[8,768,384]{2,1,0:T(8,128)(2,1)} %param.5, pred[8,768]{1,0:T(8,128)(4,1)S(1)} %iota_compare_fusion.7), kind=kOutput, calls=%fused_computation.4 | convolution fusion | flops 3628597248 | bytes 18880512 | tf_op jit(solution)/shard_map/sab,sbc->sac/dot_general | solution.py:121
  32.2 5.8 %convert_bitcast_fusion.half_ref = bf16[8,768,384]{2,1,0:T(8,128)(2,1)} fusion(bf16[8,768,384]{1,2,0:T(8,128)(2,1)S(1)} %convert_bitcast_fusion.1, s32[768]{0:T(1024)S(1)} %fusion.35), kind=kOutput, calls=%fused_computation.3 | convolution fusion | flops 3626827776 | bytes 9440256 | tf_op jit(solution)/shard_map/ia,sac->sic/dot_general | solution.py:127
  38.0 0.2 select_reduce_fusion
  38.3 69.3 %collective-permute-done.comp_ref = bf16[1,384,384]{2,1,0:T(8,128)(2,1)} collective-permute-done((bf16[1,384,384]{2,1,0:T(8,128)(2,1)}, bf16[1,384,384]{2,1,0:T(8,128)(2,1)}, u32[]{:S(2)}, u32[]{:S(2)}) %collective-permute-start) | collective-permute-done | bytes 294944 | tf_op jit(solution)/shard_map/ppermute | solution.py:99
  107.6 5.1 %collective-permute-start.18 = (bf16[1,384,384]{2,1,0:T(8,128)(2,1)S(1)}, bf16[1,384,384]{2,1,0:T(8,128)(2,1)}, u32[]{:S(2)}, u32[]{:S(2)}) collective-permute-start(bf16[1,384,384]{2,1,0:T(8,128)(2,1)S(1)} %get-tuple-element.46), channel_id=1, source_target_pairs={{0,252},{4,248},{8,244},{12,240},{16,236},{20,232},{24,228},{28,22... | collective-permute-start | bytes 884744 | tf_op jit(solution)/shard_map/ppermute | solution.py:99
  112.7 2.5 %terms.6 = (f32[1,384,384]{2,1,0:T(8,128)}, bf16[1,384,384]{2,1,0:T(8,128)(2,1)}) custom-call(bf16[8,768,384]{2,1,0:T(8,128)(2,1)} %convert_bitcast_fusion.half_ref, bf16[1,384,384]{2,1,0:T(8,128)(2,1)} %collective-permute-done.comp_ref), custom_call_target="tpu_custom_call" | custom-call | tf_op jit(solution)/shard_map/terms/pallas_call | solution.py:81
  115.2 2.5 %terms.7 = (f32[1,384,384]{2,1,0:T(8,128)}, bf16[1,384,384]{2,1,0:T(8,128)(2,1)}) custom-call(bf16[8,768,384]{2,1,0:T(8,128)(2,1)} %convert_bitcast_fusion.half_ref, bf16[1,384,384]{2,1,0:T(8,128)(2,1)} %collective-permute-done.3.comp_ref), custom_call_target="tpu_custom_call" | custom-call | tf_op jit(solution)/shard_map/terms/pallas_call | solution.py:81
  117.8 1.7 collective-permute-start.1
  119.5 2.7 %fusion.13.half_ref = bf16[1,768,384]{2,1,0:T(8,128)(2,1)} fusion(s32[768]{0:T(1024)S(1)} %fusion.46, bf16[8,768,384]{1,2,0:T(8,128)(2,1)} %copy-done.15), kind=kOutput, calls=%fused_computation.14 | convolution fusion | flops 453869568 | bytes 1182720 | tf_op jit(solution)/shard_map/ia,sac->sic/dot_general | solution.py:127
  122.2 3.1 %terms.8 = (f32[2,384,384]{2,1,0:T(8,128)}, bf16[2,384,384]{2,1,0:T(8,128)(2,1)}) custom-call(bf16[8,768,384]{2,1,0:T(8,128)(2,1)} %convert_bitcast_fusion.half_ref, bf16[2,384,384]{2,1,0:T(8,128)(2,1)} %copy-done.4), custom_call_target="tpu_custom_call" | custom-call | tf_op jit(solution)/shard_map/terms/pallas_call | solution.py:81
  125.3 0.9 copy-done.3
  126.2 3.1 %terms.9 = (f32[2,384,384]{2,1,0:T(8,128)}, bf16[2,384,384]{2,1,0:T(8,128)(2,1)}) custom-call(bf16[8,768,384]{2,1,0:T(8,128)(2,1)} %convert_bitcast_fusion.half_ref, bf16[2,384,384]{2,1,0:T(8,128)(2,1)} %copy-done.3), custom_call_target="tpu_custom_call" | custom-call | tf_op jit(solution)/shard_map/terms/pallas_call | solution.py:81
  129.2 2.6 %terms.10 = (f32[1,384,384]{2,1,0:T(8,128)}, bf16[1,384,384]{2,1,0:T(8,128)(2,1)}) custom-call(bf16[1,768,384]{2,1,0:T(8,128)(2,1)} %fusion.13.half_ref, bf16[1,384,384]{2,1,0:T(8,128)(2,1)} %collective-permute-done.18.comp_ref), custom_call_target="tpu_custom_call" | custom-call | tf_op jit(solution)/shard_map/terms/pallas_call | solution.py:81
  131.8 0.7 copy-done.9
  132.5 2.6 %terms.11 = (f32[1,384,384]{2,1,0:T(8,128)}, bf16[1,384,384]{2,1,0:T(8,128)(2,1)}) custom-call(bf16[8,768,384]{2,1,0:T(8,128)(2,1)} %convert_bitcast_fusion.half_ref, bf16[1,384,384]{2,1,0:T(8,128)(2,1)} %copy-done.9), custom_call_target="tpu_custom_call" | custom-call | tf_op jit(solution)/shard_map/terms/pallas_call | solution.py:81
  135.3 0.1 collective-permute-start.5
  135.5 1.5 collective-permute-start.2
  137.0 2.3 %collective-permute-done.5 = bf16[1,192,384]{2,1,0:T(8,128)(2,1)S(1)} collective-permute-done((bf16[1,192,384]{2,1,0:T(8,128)(2,1)S(1)}, bf16[1,192,384]{2,1,0:T(8,128)(2,1)S(1)}, u32[]{:S(2)}, u32[]{:S(2)}) %collective-permute-start.5) | collective-permute-done | bytes 147488 | tf_op jit(solution)/shard_map/ppermute | solution.py:99
  139.4 2.2 collective-permute-done.2
  141.7 0.1 collective-permute-start.8
  141.8 2.6 %collective-permute-start.7 = (bf16[2,48,384]{2,1,0:T(8,128)(2,1)S(1)}, bf16[2,48,384]{2,1,0:T(8,128)(2,1)S(1)}, u32[]{:S(2)}, u32[]{:S(2)}) collective-permute-start(bf16[2,48,384]{2,1,0:T(8,128)(2,1)S(1)} %get-tuple-element.54), channel_id=1, source_target_pairs={{0,192},{4,196},{8,200},{12,204},{16,208},{20,212},{24,216},{28,22... | collective-permute-start | bytes 221192 | tf_op jit(solution)/shard_map/ppermute | solution.py:99
  144.4 1.2 collective-permute-start.6
  145.6 0.5 collective-permute-start.19
  146.1 0.9 collective-permute-done.8
  147.1 1.5 collective-permute-start.13
  148.7 0.5 collective-permute-start.23
  149.2 2.4 %collective-permute-done.19 = bf16[1,384,384]{2,1,0:T(8,128)(2,1)S(1)} collective-permute-done((bf16[1,384,384]{2,1,0:T(8,128)(2,1)S(1)}, bf16[1,384,384]{2,1,0:T(8,128)(2,1)S(1)}, u32[]{:S(2)}, u32[]{:S(2)}) %collective-permute-start.19) | collective-permute-done | bytes 294944 | tf_op jit(solution)/shard_map/ppermute | solution.py:99
  151.7 0.1 collective-permute-start.20
  151.8 1.6 collective-permute-done.23
  153.4 4.1 %collective-permute-done.16 = bf16[2,384,384]{2,1,0:T(8,128)(2,1)S(1)} collective-permute-done((bf16[2,384,384]{2,1,0:T(8,128)(2,1)S(1)}, bf16[2,384,384]{2,1,0:T(8,128)(2,1)S(1)}, u32[]{:S(2)}, u32[]{:S(2)}) %collective-permute-start.16) | collective-permute-done | bytes 589856 | tf_op jit(solution)/shard_map/ppermute | solution.py:99
  157.5 0.1 convert_add_fusion
  157.6 0.8 collective-permute-start.17
  158.5 11.6 %collective-permute-done.13 = bf16[2,384,384]{2,1,0:T(8,128)(2,1)S(1)} collective-permute-done((bf16[2,384,384]{2,1,0:T(8,128)(2,1)S(1)}, bf16[2,384,384]{2,1,0:T(8,128)(2,1)S(1)}, u32[]{:S(2)}, u32[]{:S(2)}) %collective-permute-start.13) | collective-permute-done | bytes 589856 | tf_op jit(solution)/shard_map/ppermute | solution.py:99
  170.1 0.1 convert_add_fusion.1
  170.3 0.8 collective-permute-start.14
  171.1 2.2 %collective-permute-done.20 = bf16[1,192,384]{2,1,0:T(8,128)(2,1)S(1)} collective-permute-done((bf16[1,192,384]{2,1,0:T(8,128)(2,1)S(1)}, bf16[1,192,384]{2,1,0:T(8,128)(2,1)S(1)}, u32[]{:S(2)}, u32[]{:S(2)}) %collective-permute-start.20) | collective-permute-done | bytes 147488 | tf_op jit(solution)/shard_map/ppermute | solution.py:99
  173.4 4.0 %collective-permute-done.14 = bf16[2,192,384]{2,1,0:T(8,128)(2,1)S(1)} collective-permute-done((bf16[2,192,384]{2,1,0:T(8,128)(2,1)S(1)}, bf16[2,192,384]{2,1,0:T(8,128)(2,1)S(1)}, u32[]{:S(2)}, u32[]{:S(2)}) %collective-permute-start.14) | collective-permute-done | bytes 294944 | tf_op jit(solution)/shard_map/ppermute | solution.py:99
  177.5 0.2 fusion.55
  177.8 0.4 collective-permute-start.26
  178.2 2.3 %collective-permute-start.25 = (bf16[6,48,384]{2,1,0:T(8,128)(2,1)S(1)}, bf16[6,48,384]{2,1,0:T(8,128)(2,1)S(1)}, u32[]{:S(2)}, u32[]{:S(2)}) collective-permute-start(bf16[6,48,384]{2,1,0:T(8,128)(2,1)S(1)} %get-tuple-element.51), channel_id=1, source_target_pairs={{0,192},{4,196},{8,200},{12,204},{16,208},{20,212},{24,216},{28,22... | collective-permute-start | bytes 663560 | tf_op jit(solution)/shard_map/ppermute | solution.py:99
  180.5 1.2 collective-permute-start.24
  181.7 0.1 collective-permute-start.11
  181.8 3.8 %collective-permute-start.10 = (bf16[2,12,384]{2,1,0:T(8,128)(2,1)S(1)}, bf16[2,12,384]{2,1,0:T(8,128)(2,1)S(1)}, u32[]{:S(2)}, u32[]{:S(2)}) collective-permute-start(bf16[2,12,384]{2,1,0:T(8,128)(2,1)S(1)} %get-tuple-element.60), channel_id=1, source_target_pairs={{0,32},{4,36},{8,40},{12,44},{16,48},{20,52},{24,56},{28,60},{32,0... | collective-permute-start | bytes 55304 | tf_op jit(solution)/shard_map/ppermute | solution.py:99
  185.6 0.1 pad_maximum_fusion
  185.8 1.9 collective-permute-start.9
  187.7 0.1 fusion.58
  187.9 0.2 collective-permute-start.29
  188.1 3.7 %collective-permute-start.28 = (bf16[6,12,384]{2,1,0:T(8,128)(2,1)S(1)}, bf16[6,12,384]{2,1,0:T(8,128)(2,1)S(1)}, u32[]{:S(2)}, u32[]{:S(2)}) collective-permute-start(bf16[6,12,384]{2,1,0:T(8,128)(2,1)S(1)} %get-tuple-element.57), channel_id=1, source_target_pairs={{0,32},{4,36},{8,40},{12,44},{16,48},{20,52},{24,56},{28,60},{32,0... | collective-permute-start | bytes 165896 | tf_op jit(solution)/shard_map/ppermute | solution.py:99
  191.8 1.9 collective-permute-start.27
  193.7 1.8 collective-permute-done.28
  195.4 3.1 %collective-permute-done.27 = bf16[6,12,384]{2,1,0:T(8,128)(2,1)S(1)} collective-permute-done((bf16[6,12,384]{2,1,0:T(8,128)(2,1)S(1)}, bf16[6,12,384]{2,1,0:T(8,128)(2,1)S(1)}, u32[]{:S(2)}, u32[]{:S(2)}) %collective-permute-start.27) | collective-permute-done | bytes 55328 | tf_op jit(solution)/shard_map/ppermute | solution.py:99
  198.6 16.0 %all_gather.3 = bf16[32,12,384]{2,0,1:T(8,128)(2,1)S(1)} all-gather(bf16[8,12,384]{2,0,1:T(8,128)(2,1)S(1)} %copy.23), channel_id=1, replica_groups=mesh['pair'=64,'sec'=4] {'sec'}, dimensions={0}, use_global_device_ids=true | all-gather | bytes 368640 | tf_op jit(solution)/shard_map/all_gather | solution.py:158
  214.6 0.1 copy.24
  214.8 0.6 gather_fusion
  215.3 0.1 broadcast_select_fusion
  215.4 0.6 copy.25
  (85 shorter events, 1.3 us)
Async XLA Ops:
  0.0 12.0 %copy-start = (bf16[1,8,384,384]{3,2,1,0:T(8,128)(2,1)S(1)}, bf16[1,8,384,384]{3,2,1,0:T(8,128)(2,1)}, u32[]{:S(2)}) copy-start(bf16[1,8,384,384]{3,2,1,0:T(8,128)(2,1)} %param.9) | copy-start | bytes 7077892
  0.0 23.6 %copy-start.13 = (s32[32]{0:T(128)S(1)}, s32[32]{0:T(128)}, u32[]{:S(2)}) copy-start(s32[32]{0:T(128)} %param.6) | copy-start | bytes 388
  2.2 129.6 %collective-permute-start.21 = (bf16[1,384,384]{2,1,0:T(8,128)(2,1)S(1)}, bf16[1,384,384]{2,1,0:T(8,128)(2,1)S(1)}, u32[]{:S(2)}, u32[]{:S(2)}) collective-permute-start(bf16[1,384,384]{2,1,0:T(8,128)(2,1)S(1)} %get-tuple-element.45), channel_id=1, source_target_pairs={{0,252},{4,248},{8,244},{12,240},{16,236},{20,232},{24,228},{28,22... | collective-permute-start | bytes 884744 | tf_op jit(solution)/shard_map/ppermute | solution.py:99
  12.1 113.2 %collective-permute-start.15 = (bf16[2,384,384]{2,1,0:T(8,128)(2,1)S(1)}, bf16[2,384,384]{2,1,0:T(8,128)(2,1)S(1)}, u32[]{:S(2)}, u32[]{:S(2)}) collective-permute-start(bf16[2,384,384]{2,1,0:T(8,128)(2,1)S(1)} %get-tuple-element.48), channel_id=1, source_target_pairs={{0,252},{4,248},{8,244},{12,240},{16,236},{20,232},{24,228},{28,22... | collective-permute-start | bytes 1769480 | tf_op jit(solution)/shard_map/ppermute | solution.py:99
  12.2 105.5 %collective-permute-start.12 = (bf16[2,384,384]{2,1,0:T(8,128)(2,1)S(1)}, bf16[2,384,384]{2,1,0:T(8,128)(2,1)S(1)}, u32[]{:S(2)}, u32[]{:S(2)}) collective-permute-start(bf16[2,384,384]{2,1,0:T(8,128)(2,1)S(1)} %get-tuple-element.47), channel_id=1, source_target_pairs={{0,252},{4,248},{8,244},{12,240},{16,236},{20,232},{24,228},{28,22... | collective-permute-start | bytes 1769480 | tf_op jit(solution)/shard_map/ppermute | solution.py:99
  17.9 97.3 %collective-permute-start.3 = (bf16[1,384,384]{2,1,0:T(8,128)(2,1)S(1)}, bf16[1,384,384]{2,1,0:T(8,128)(2,1)}, u32[]{:S(2)}, u32[]{:S(2)}) collective-permute-start(bf16[1,384,384]{2,1,0:T(8,128)(2,1)S(1)} %get-tuple-element.44), channel_id=1, source_target_pairs={{0,252},{4,248},{8,244},{12,240},{16,236},{20,232},{24,228},{28,22... | collective-permute-start | bytes 884744 | tf_op jit(solution)/shard_map/ppermute | solution.py:99
  18.0 89.6 %collective-permute-start = (bf16[1,384,384]{2,1,0:T(8,128)(2,1)}, bf16[1,384,384]{2,1,0:T(8,128)(2,1)}, u32[]{:S(2)}, u32[]{:S(2)}) collective-permute-start(bf16[1,384,384]{2,1,0:T(8,128)(2,1)} %get-tuple-element.43), channel_id=1, source_target_pairs={{0,252},{4,248},{8,244},{12,240},{16,236},{20,232},{24,228},{28,22... | collective-permute-start | bytes 884744 | tf_op jit(solution)/shard_map/ppermute | solution.py:99
  32.1 5.8 %copy-start.15 = (bf16[8,768,384]{1,2,0:T(8,128)(2,1)}, bf16[8,768,384]{1,2,0:T(8,128)(2,1)S(1)}, u32[]{:S(2)}) copy-start(bf16[8,768,384]{1,2,0:T(8,128)(2,1)S(1)} %convert_bitcast_fusion.1) | copy-start | bytes 14155780
  32.2 5.8 %copy-start.14 = (s32[32]{0:T(128)S(1)}, s32[32]{0:T(128)}, u32[]{:S(2)}) copy-start(s32[32]{0:T(128)} %param.7) | copy-start | bytes 388
  107.6 21.6 %collective-permute-start.18 = (bf16[1,384,384]{2,1,0:T(8,128)(2,1)S(1)}, bf16[1,384,384]{2,1,0:T(8,128)(2,1)}, u32[]{:S(2)}, u32[]{:S(2)}) collective-permute-start(bf16[1,384,384]{2,1,0:T(8,128)(2,1)S(1)} %get-tuple-element.46), channel_id=1, source_target_pairs={{0,252},{4,248},{8,244},{12,240},{16,236},{20,232},{24,228},{28,22... | collective-permute-start | bytes 884744 | tf_op jit(solution)/shard_map/ppermute | solution.py:99
  117.7 17.4 %collective-permute-start.4 = (bf16[1,384,384]{2,1,0:T(8,128)(2,1)}, bf16[1,384,384]{2,1,0:T(8,128)(2,1)S(1)}, u32[]{:S(2)}, u32[]{:S(2)}) collective-permute-start(bf16[1,384,384]{2,1,0:T(8,128)(2,1)} %get-tuple-element.26), channel_id=1, source_target_pairs={{0,64},{4,68},{8,72},{12,76},{16,80},{20,84},{24,88},{28,92},{32,9... | collective-permute-start | bytes 884744 | tf_op jit(solution)/shard_map/ppermute | solution.py:99
  117.8 4.4 %copy-start.4 = (bf16[2,384,384]{2,1,0:T(8,128)(2,1)}, bf16[2,384,384]{2,1,0:T(8,128)(2,1)S(1)}, u32[]{:S(2)}) copy-start(bf16[2,384,384]{2,1,0:T(8,128)(2,1)S(1)} %collective-permute-done.12.comp_ref) | copy-start | bytes 1769476
  117.8 17.6 %collective-permute-start.1 = (bf16[1,384,384]{2,1,0:T(8,128)(2,1)}, bf16[1,384,384]{2,1,0:T(8,128)(2,1)S(1)}, u32[]{:S(2)}, u32[]{:S(2)}) collective-permute-start(bf16[1,384,384]{2,1,0:T(8,128)(2,1)} %get-tuple-element.23), channel_id=1, source_target_pairs={{0,64},{4,68},{8,72},{12,76},{16,80},{20,84},{24,88},{28,92},{32,9... | collective-permute-start | bytes 884744 | tf_op jit(solution)/shard_map/ppermute | solution.py:99
  125.3 0.9 copy-start.3
  131.8 0.7 copy-start.9
  132.5 2.6 %copy-start.8 = (f32[1,384,384]{2,1,0:T(8,128)S(1)}, f32[1,384,384]{2,1,0:T(8,128)}, u32[]{:S(2)}) copy-start(f32[1,384,384]{2,1,0:T(8,128)} %get-tuple-element.25) | copy-start | bytes 1769476
  132.5 2.9 %copy-start.7 = (f32[1,384,384]{2,1,0:T(8,128)S(1)}, f32[1,384,384]{2,1,0:T(8,128)}, u32[]{:S(2)}) copy-start(f32[1,384,384]{2,1,0:T(8,128)} %get-tuple-element.22) | copy-start | bytes 1769476
  135.1 13.5 %collective-permute-start.22 = (bf16[1,384,384]{2,1,0:T(8,128)(2,1)}, bf16[1,384,384]{2,1,0:T(8,128)(2,1)S(1)}, u32[]{:S(2)}, u32[]{:S(2)}) collective-permute-start(bf16[1,384,384]{2,1,0:T(8,128)(2,1)} %get-tuple-element.38), channel_id=1, source_target_pairs={{0,64},{4,68},{8,72},{12,76},{16,80},{20,84},{24,88},{28,92},{32,9... | collective-permute-start | bytes 884744 | tf_op jit(solution)/shard_map/ppermute | solution.py:99
  135.2 10.4 %copy-start.12 = (bf16[1,384,384]{2,1,0:T(8,128)(2,1)S(1)}, bf16[1,384,384]{2,1,0:T(8,128)(2,1)}, u32[]{:S(2)}) copy-start(bf16[1,384,384]{2,1,0:T(8,128)(2,1)} %get-tuple-element.35) | copy-start | bytes 884740
  135.2 11.8 %copy-start.11 = (bf16[2,384,384]{2,1,0:T(8,128)(2,1)S(1)}, bf16[2,384,384]{2,1,0:T(8,128)(2,1)}, u32[]{:S(2)}) copy-start(bf16[2,384,384]{2,1,0:T(8,128)(2,1)} %get-tuple-element.32) | copy-start | bytes 1769476
  135.2 11.8 %copy-start.10 = (bf16[2,384,384]{2,1,0:T(8,128)(2,1)S(1)}, bf16[2,384,384]{2,1,0:T(8,128)(2,1)}, u32[]{:S(2)}) copy-start(bf16[2,384,384]{2,1,0:T(8,128)(2,1)} %get-tuple-element.29) | copy-start | bytes 1769476
  135.3 4.1 %collective-permute-start.5 = (bf16[1,192,384]{2,1,0:T(8,128)(2,1)S(1)}, bf16[1,192,384]{2,1,0:T(8,128)(2,1)S(1)}, u32[]{:S(2)}, u32[]{:S(2)}) collective-permute-start(bf16[1,192,384]{2,1,0:T(8,128)(2,1)S(1)} %slice.229), channel_id=1, source_target_pairs={{0,8},{4,12},{8,0},{12,4},{16,24},{20,28},{24,16},{28,20},{32,40},... | collective-permute-start | bytes 442376 | tf_op jit(solution)/shard_map/ppermute | solution.py:99
  135.4 13.2 %copy-start.6 = (f32[1,384,384]{2,1,0:T(8,128)S(1)}, f32[1,384,384]{2,1,0:T(8,128)}, u32[]{:S(2)}) copy-start(f32[1,384,384]{2,1,0:T(8,128)} %get-tuple-element.37) | copy-start | bytes 1769476
  135.5 6.1 %collective-permute-start.2 = (bf16[1,192,384]{2,1,0:T(8,128)(2,1)S(1)}, bf16[1,192,384]{2,1,0:T(8,128)(2,1)S(1)}, u32[]{:S(2)}, u32[]{:S(2)}) collective-permute-start(bf16[1,192,384]{2,1,0:T(8,128)(2,1)S(1)} %slice.230), channel_id=1, source_target_pairs={{0,8},{4,12},{8,0},{12,4},{16,24},{20,28},{24,16},{28,20},{32,40},... | collective-permute-start | bytes 442376 | tf_op jit(solution)/shard_map/ppermute | solution.py:99
  139.4 12.2 %copy-start.5 = (f32[1,384,384]{2,1,0:T(8,128)S(1)}, f32[1,384,384]{2,1,0:T(8,128)}, u32[]{:S(2)}) copy-start(f32[1,384,384]{2,1,0:T(8,128)} %get-tuple-element.34) | copy-start | bytes 1769476
  141.7 5.4 %collective-permute-start.8 = (bf16[2,48,384]{2,1,0:T(8,128)(2,1)S(1)}, bf16[2,48,384]{2,1,0:T(8,128)(2,1)S(1)}, u32[]{:S(2)}, u32[]{:S(2)}) collective-permute-start(bf16[2,48,384]{2,1,0:T(8,128)(2,1)S(1)} %get-tuple-element.53), channel_id=1, source_target_pairs={{0,196},{4,192},{8,204},{12,200},{16,212},{20,208},{24,220},{28,21... | collective-permute-start | bytes 221192 | tf_op jit(solution)/shard_map/ppermute | solution.py:99
  141.8 5.3 %collective-permute-start.7 = (bf16[2,48,384]{2,1,0:T(8,128)(2,1)S(1)}, bf16[2,48,384]{2,1,0:T(8,128)(2,1)S(1)}, u32[]{:S(2)}, u32[]{:S(2)}) collective-permute-start(bf16[2,48,384]{2,1,0:T(8,128)(2,1)S(1)} %get-tuple-element.54), channel_id=1, source_target_pairs={{0,192},{4,196},{8,200},{12,204},{16,208},{20,212},{24,216},{28,22... | collective-permute-start | bytes 221192 | tf_op jit(solution)/shard_map/ppermute | solution.py:99
  144.4 4.1 %collective-permute-start.6 = (bf16[2,48,384]{2,1,0:T(8,128)(2,1)S(1)}, bf16[2,48,384]{2,1,0:T(8,128)(2,1)S(1)}, u32[]{:S(2)}, u32[]{:S(2)}) collective-permute-start(bf16[2,48,384]{2,1,0:T(8,128)(2,1)S(1)} %get-tuple-element.52), channel_id=1, source_target_pairs={{0,4},{4,0},{8,12},{12,8},{16,20},{20,16},{24,28},{28,24},{32,36},... | collective-permute-start | bytes 221192 | tf_op jit(solution)/shard_map/ppermute | solution.py:99
  145.6 6.0 %collective-permute-start.19 = (bf16[1,384,384]{2,1,0:T(8,128)(2,1)S(1)}, bf16[1,384,384]{2,1,0:T(8,128)(2,1)S(1)}, u32[]{:S(2)}, u32[]{:S(2)}) collective-permute-start(bf16[1,384,384]{2,1,0:T(8,128)(2,1)S(1)} %copy-done.12), channel_id=1, source_target_pairs={{0,8},{4,12},{8,0},{12,4},{16,24},{20,28},{24,16},{28,20},{32,40},... | collective-permute-start | bytes 884744 | tf_op jit(solution)/shard_map/ppermute | solution.py:99
  147.1 10.4 %collective-permute-start.16 = (bf16[2,384,384]{2,1,0:T(8,128)(2,1)S(1)}, bf16[2,384,384]{2,1,0:T(8,128)(2,1)S(1)}, u32[]{:S(2)}, u32[]{:S(2)}) collective-permute-start(bf16[2,384,384]{2,1,0:T(8,128)(2,1)S(1)} %copy-done.11), channel_id=1, source_target_pairs={{0,64},{4,68},{8,72},{12,76},{16,80},{20,84},{24,88},{28,92},{32,9... | collective-permute-start | bytes 1769480 | tf_op jit(solution)/shard_map/ppermute | solution.py:99
  147.1 23.0 %collective-permute-start.13 = (bf16[2,384,384]{2,1,0:T(8,128)(2,1)S(1)}, bf16[2,384,384]{2,1,0:T(8,128)(2,1)S(1)}, u32[]{:S(2)}, u32[]{:S(2)}) collective-permute-start(bf16[2,384,384]{2,1,0:T(8,128)(2,1)S(1)} %copy-done.10), channel_id=1, source_target_pairs={{0,64},{4,68},{8,72},{12,76},{16,80},{20,84},{24,88},{28,92},{32,9... | collective-permute-start | bytes 1769480 | tf_op jit(solution)/shard_map/ppermute | solution.py:99
  148.6 8.9 %copy-start.2 = (f32[2,384,384]{2,1,0:T(8,128)S(1)}, f32[2,384,384]{2,1,0:T(8,128)}, u32[]{:S(2)}) copy-start(f32[2,384,384]{2,1,0:T(8,128)} %get-tuple-element.31) | copy-start | bytes 3538948
  148.7 4.7 %collective-permute-start.23 = (bf16[1,192,384]{2,1,0:T(8,128)(2,1)S(1)}, bf16[1,192,384]{2,1,0:T(8,128)(2,1)S(1)}, u32[]{:S(2)}, u32[]{:S(2)}) collective-permute-start(bf16[1,192,384]{2,1,0:T(8,128)(2,1)S(1)} %slice.227), channel_id=1, source_target_pairs={{0,8},{4,12},{8,0},{12,4},{16,24},{20,28},{24,16},{28,20},{32,40},... | collective-permute-start | bytes 442376 | tf_op jit(solution)/shard_map/ppermute | solution.py:99
  151.6 18.5 %copy-start.1 = (f32[2,384,384]{2,1,0:T(8,128)S(1)}, f32[2,384,384]{2,1,0:T(8,128)}, u32[]{:S(2)}) copy-start(f32[2,384,384]{2,1,0:T(8,128)} %get-tuple-element.28) | copy-start | bytes 3538948
  151.7 21.6 %collective-permute-start.20 = (bf16[1,192,384]{2,1,0:T(8,128)(2,1)S(1)}, bf16[1,192,384]{2,1,0:T(8,128)(2,1)S(1)}, u32[]{:S(2)}, u32[]{:S(2)}) collective-permute-start(bf16[1,192,384]{2,1,0:T(8,128)(2,1)S(1)} %slice.228), channel_id=1, source_target_pairs={{0,64},{4,68},{8,72},{12,76},{16,80},{20,84},{24,88},{28,92},{32,9... | collective-permute-start | bytes 442376 | tf_op jit(solution)/shard_map/ppermute | solution.py:99
  157.6 15.7 %collective-permute-start.17 = (bf16[2,192,384]{2,1,0:T(8,128)(2,1)S(1)}, bf16[2,192,384]{2,1,0:T(8,128)(2,1)S(1)}, u32[]{:S(2)}, u32[]{:S(2)}) collective-permute-start(bf16[2,192,384]{2,1,0:T(8,128)(2,1)S(1)} %slice.225), channel_id=1, source_target_pairs={{0,8},{4,12},{8,0},{12,4},{16,24},{20,28},{24,16},{28,20},{32,40},... | collective-permute-start | bytes 884744 | tf_op jit(solution)/shard_map/ppermute | solution.py:99
  170.3 7.2 %collective-permute-start.14 = (bf16[2,192,384]{2,1,0:T(8,128)(2,1)S(1)}, bf16[2,192,384]{2,1,0:T(8,128)(2,1)S(1)}, u32[]{:S(2)}, u32[]{:S(2)}) collective-permute-start(bf16[2,192,384]{2,1,0:T(8,128)(2,1)S(1)} %slice.226), channel_id=1, source_target_pairs={{0,8},{4,12},{8,0},{12,4},{16,24},{20,28},{24,16},{28,20},{32,40},... | collective-permute-start | bytes 884744 | tf_op jit(solution)/shard_map/ppermute | solution.py:99
  177.8 8.0 %collective-permute-start.26 = (bf16[6,48,384]{2,1,0:T(8,128)(2,1)S(1)}, bf16[6,48,384]{2,1,0:T(8,128)(2,1)S(1)}, u32[]{:S(2)}, u32[]{:S(2)}) collective-permute-start(bf16[6,48,384]{2,1,0:T(8,128)(2,1)S(1)} %get-tuple-element.50), channel_id=1, source_target_pairs={{0,196},{4,192},{8,204},{12,200},{16,212},{20,208},{24,220},{28,21... | collective-permute-start | bytes 663560 | tf_op jit(solution)/shard_map/ppermute | solution.py:99
  178.2 9.5 %collective-permute-start.25 = (bf16[6,48,384]{2,1,0:T(8,128)(2,1)S(1)}, bf16[6,48,384]{2,1,0:T(8,128)(2,1)S(1)}, u32[]{:S(2)}, u32[]{:S(2)}) collective-permute-start(bf16[6,48,384]{2,1,0:T(8,128)(2,1)S(1)} %get-tuple-element.51), channel_id=1, source_target_pairs={{0,192},{4,196},{8,200},{12,204},{16,208},{20,212},{24,216},{28,22... | collective-permute-start | bytes 663560 | tf_op jit(solution)/shard_map/ppermute | solution.py:99
  180.5 7.2 %collective-permute-start.24 = (bf16[6,48,384]{2,1,0:T(8,128)(2,1)S(1)}, bf16[6,48,384]{2,1,0:T(8,128)(2,1)S(1)}, u32[]{:S(2)}, u32[]{:S(2)}) collective-permute-start(bf16[6,48,384]{2,1,0:T(8,128)(2,1)S(1)} %get-tuple-element.49), channel_id=1, source_target_pairs={{0,4},{4,0},{8,12},{12,8},{16,20},{20,16},{24,28},{28,24},{32,36},... | collective-permute-start | bytes 663560 | tf_op jit(solution)/shard_map/ppermute | solution.py:99
  181.7 10.0 %collective-permute-start.11 = (bf16[2,12,384]{2,1,0:T(8,128)(2,1)S(1)}, bf16[2,12,384]{2,1,0:T(8,128)(2,1)S(1)}, u32[]{:S(2)}, u32[]{:S(2)}) collective-permute-start(bf16[2,12,384]{2,1,0:T(8,128)(2,1)S(1)} %get-tuple-element.59), channel_id=1, source_target_pairs={{0,48},{4,52},{8,56},{12,60},{16,32},{20,36},{24,40},{28,44},{32,1... | collective-permute-start | bytes 55304 | tf_op jit(solution)/shard_map/ppermute | solution.py:99
  181.8 11.8 %collective-permute-start.10 = (bf16[2,12,384]{2,1,0:T(8,128)(2,1)S(1)}, bf16[2,12,384]{2,1,0:T(8,128)(2,1)S(1)}, u32[]{:S(2)}, u32[]{:S(2)}) collective-permute-start(bf16[2,12,384]{2,1,0:T(8,128)(2,1)S(1)} %get-tuple-element.60), channel_id=1, source_target_pairs={{0,32},{4,36},{8,40},{12,44},{16,48},{20,52},{24,56},{28,60},{32,0... | collective-permute-start | bytes 55304 | tf_op jit(solution)/shard_map/ppermute | solution.py:99
  185.8 7.9 %collective-permute-start.9 = (bf16[2,12,384]{2,1,0:T(8,128)(2,1)S(1)}, bf16[2,12,384]{2,1,0:T(8,128)(2,1)S(1)}, u32[]{:S(2)}, u32[]{:S(2)}) collective-permute-start(bf16[2,12,384]{2,1,0:T(8,128)(2,1)S(1)} %get-tuple-element.58), channel_id=1, source_target_pairs={{0,16},{4,20},{8,24},{12,28},{16,0},{20,4},{24,8},{28,12},{32,48},... | collective-permute-start | bytes 55304 | tf_op jit(solution)/shard_map/ppermute | solution.py:99
  187.9 5.8 %collective-permute-start.29 = (bf16[6,12,384]{2,1,0:T(8,128)(2,1)S(1)}, bf16[6,12,384]{2,1,0:T(8,128)(2,1)S(1)}, u32[]{:S(2)}, u32[]{:S(2)}) collective-permute-start(bf16[6,12,384]{2,1,0:T(8,128)(2,1)S(1)} %get-tuple-element.56), channel_id=1, source_target_pairs={{0,48},{4,52},{8,56},{12,60},{16,32},{20,36},{24,40},{28,44},{32,1... | collective-permute-start | bytes 165896 | tf_op jit(solution)/shard_map/ppermute | solution.py:99
  188.1 7.4 %collective-permute-start.28 = (bf16[6,12,384]{2,1,0:T(8,128)(2,1)S(1)}, bf16[6,12,384]{2,1,0:T(8,128)(2,1)S(1)}, u32[]{:S(2)}, u32[]{:S(2)}) collective-permute-start(bf16[6,12,384]{2,1,0:T(8,128)(2,1)S(1)} %get-tuple-element.57), channel_id=1, source_target_pairs={{0,32},{4,36},{8,40},{12,44},{16,48},{20,52},{24,56},{28,60},{32,0... | collective-permute-start | bytes 165896 | tf_op jit(solution)/shard_map/ppermute | solution.py:99
  191.8 6.7 %collective-permute-start.27 = (bf16[6,12,384]{2,1,0:T(8,128)(2,1)S(1)}, bf16[6,12,384]{2,1,0:T(8,128)(2,1)S(1)}, u32[]{:S(2)}, u32[]{:S(2)}) collective-permute-start(bf16[6,12,384]{2,1,0:T(8,128)(2,1)S(1)} %get-tuple-element.55), channel_id=1, source_target_pairs={{0,16},{4,20},{8,24},{12,28},{16,0},{20,4},{24,8},{28,12},{32,48},... | collective-permute-start | bytes 165896 | tf_op jit(solution)/shard_map/ppermute | solution.py:99

commit v2 on v1

--- a/solution.py
+++ b/solution.py
@@ -8,7 +8,7 @@
 INTERPRET = False
 YS, ZS, XS = 4, 8, 2
 CHUNKS = ((0, 1), (1, 2), (2, 4), (4, 6), (6, 7), (7, 8))
-GROUPS = ((0, 1), (2, 3, 4, 5))
+GROUPS = ((0, 1), (2, 3), (4, 5))
 SWAPPED = (4,)
 F32, BF16 = jnp.float32, jnp.bfloat16
 
@@ -95,6 +95,29 @@
     )(half, comp)
 
 
+def part_kernel(half_ref, comp_ref, out_ref):
+    out_ref[0] = lax.dot_general(
+        half_ref[0], comp_ref[0], (((1,), (1,)), ((), ())), preferred_element_type=F32
+    ).astype(out_ref.dtype)
+
+
+def part_of(half, comp, start, part, dtype):
+    sectors, cols, _ = comp.shape
+    rows = half.shape[1] // 2
+    return pl.pallas_call(
+        part_kernel,
+        grid=(sectors,),
+        in_specs=[
+            pl.BlockSpec((1, rows, cols), lambda s: (s + start, part, 0)),
+            pl.BlockSpec((1, cols, cols), lambda s: (s, 0, 0)),
+        ],
+        out_specs=pl.BlockSpec((1, rows, cols), lambda s: (s, 0, 0)),
+        out_shape=jax.ShapeDtypeStruct((sectors, rows, cols), dtype),
+        interpret=INTERPRET,
+        name="part",
+    )(half, comp)
+
+
 def exchange(value, perm):
     return lax.ppermute(value, "pair", perm)
 
@@ -114,7 +137,14 @@
     targets = first_sec + jnp.arange(sec_dev, dtype=jnp.int32)
     rows_here = lax.dynamic_slice_in_dim(sec_rows, first_sec, sec_dev)
 
-    mirrored = [exchange(comp_ops[0, a:b], MIRROR) for a, b in CHUNKS]
+    mirrored = []
+    blocks, rest = comp_ops[0, : CHUNKS[0][1]], comp_ops[0]
+    for i, (a, b) in enumerate(CHUNKS):
+        if i:
+            blocks = rest[a:b]
+        mirrored.append(exchange(blocks, MIRROR))
+        if not i:
+            rest, _ = lax.optimization_barrier((rest, blocks))
 
     line = jnp.arange(block_rows, dtype=jnp.int32)
     kept = jnp.where((line[None, :] < rows_here[:, None])[:, :, None], psi, jnp.zeros_like(psi))
@@ -133,28 +163,32 @@
         if i:
             comp, _ = lax.optimization_barrier((comp, flows[-1][1]))
         source, start = routed[i in SWAPPED]
-        flows.append(terms_of(source, comp, a - start))
-    pieces = []
+        if i + 1 < len(CHUNKS):
+            flows.append(terms_of(source, comp, a - start))
+        else:
+            send = part_of(source, comp, a - start, 1, BF16)
+    flows.append((part_of(source, comp, a - start, 0, F32), send))
+    def swap_four(perms, total):
+        cut = total.shape[1] // 4
+        got = [
+            exchange(total[:, (n + 1) * cut : (n + 2) * cut].astype(BF16), perms[n])
+            for n in range(3)
+        ]
+        return total[:, :cut] + sum(value.astype(F32) for value in got)
+
+    totals = []
     for group in GROUPS:
         parts = []
         for i in group:
+            near, far = "ba" if i in SWAPPED else "ab"
             keep, send = flows[i]
-            near, far = "ba" if i in SWAPPED else "ab"
             got = exchange(send, STAGES[near])
             keep, send = fold(keep, got)
             got = exchange(send, STAGES[far])
             parts.append(keep + got.astype(F32))
-        total = jnp.concatenate(parts, axis=0)
-        for stage in "ce":
-            cut = total.shape[1] // 4
-            got = [
-                exchange(total[:, (n + 1) * cut : (n + 2) * cut].astype(BF16), FOURS[stage][n])
-                for n in range(3)
-            ]
-            total = total[:, :cut] + sum(value.astype(F32) for value in got)
-        pieces.append(total.astype(BF16))
-
-    partial_rows = jnp.concatenate(pieces, axis=0)
+        totals.append(swap_four(FOURS["c"], jnp.concatenate(parts, axis=0)))
+    total = swap_four(FOURS["e"], jnp.concatenate(totals, axis=0))
+    partial_rows = total.astype(BF16)
     gathered = lax.all_gather(partial_rows, "sec", axis=0, tiled=True)
     summed = pick_sources(gathered, match, targets)
     my_lines = pair * share + jnp.arange(share, dtype=jnp.int32)

time: 216 us -> 235 us (1.088)
  waiting for transfers between devices: 106 us -> 120 us
  local copies, waits for them, and re-layouts: 5.69 us -> 9.89 us
  starting transfers between devices: 53.4 us -> 50.7 us
    ppermute x30, waiting for transfers between devices: 106 us -> 120 us  [exchange(): return lax.ppermute(value, 'pair', perm)]
    pallas_call x0 -> x2, Pallas kernels: none -> 4.47 us  [part_of(): pl.pallas_call(part_kernel, grid=(sectors,), in_specs=[pl.BlockSpec((1, r...]
    ppermute x30, starting transfers between devices: 53.4 us -> 50.7 us  [exchange(): return lax.ppermute(value, 'pair', perm)]
    pallas_call x6 -> x5, Pallas kernels: 16.3 us -> 13.8 us  [terms_of(): pl.pallas_call(terms_kernel, grid=(sectors,), in_specs=[pl.BlockSpec((1,...]
    unnamed x32 -> x38, local copies, waits for them, and re-layouts: 1.63 us -> 4.12 us
  transfers between devices with their start and end apart: 30 -> 30, of which waited for: 12 -> 14; matrix products, arithmetic and copies ran while one was open for 9% -> 9% of each run, Pallas kernels for 8% -> 8%
where the time goes in v2:
time: 235 us
  waiting for transfers between devices  120 us (51%)
  starting transfers between devices  50.7 us (22%)
  Pallas kernels  18.3 us (8%)
  matrix products  16.8 us (7%)
  blocking collectives  15.9 us (7%)
  local copies, waits for them, and re-layouts  9.89 us (4%)
  other arithmetic  3.08 us (1%)
    ppermute x30, waiting for transfers between devices, exchange(): return lax.ppermute(value, 'pair', perm)  120 us
    ppermute x30, starting transfers between devices, exchange(): return lax.ppermute(value, 'pair', perm)  50.7 us
    all_gather x1, blocking collectives, product(): gathered = lax.all_gather(partial_rows, 'sec', axis=0, tiled=True)  15.9 us
    pallas_call x5, Pallas kernels, terms_of(): pl.pallas_call(terms_kernel, grid=(sectors,), in_specs=[pl.BlockSpec((1,...  13.8 us
    dot_general x2, matrix products, product(): jnp.einsum('ia,sac->sic', order, half[first:end], preferred_element_type=...  8.46 us
    dot_general x1, matrix products, product(): jnp.einsum('sab,sbc->sac', normal_ops[0], kept, preferred_element_type=F32)  8.39 us
  transfers between devices with their start and end apart: 30, of which 14 were waited for; matrix products, arithmetic and copies ran while one was open for 9% of the time, Pallas kernels for 8%

profile of v2, /device:TPU:1, one launch (start us, length us, event | category | flops | bytes accessed | tf_op | source)
XLA Modules:
  0.0 234.9 jit_solution(10859275531560615082)
XLA Ops:
  0.0 1.9 slice_bitcast_fusion.2
  1.9 9.8 %collective-permute-start = (bf16[1,384,384]{2,1,0:T(8,128)(2,1)}, bf16[1,384,384]{2,1,0:T(8,128)(2,1)S(1)}, u32[]{:S(2)}, u32[]{:S(2)}) collective-permute-start(bf16[1,384,384]{2,1,0:T(8,128)(2,1)} %slice_bitcast_fusion.2), channel_id=1, source_target_pairs={{0,252},{4,248},{8,244},{12,240},{16,236},{20,232},{24,228},{28,22... | collective-permute-start | bytes 884744 | tf_op jit(solution)/shard_map/ppermute | solution.py:122
  11.6 2.1 fusion.61
  13.7 0.1 fusion.62
  13.8 5.8 %collective-permute-start.12 = (bf16[2,384,384]{2,1,0:T(8,128)(2,1)S(1)}, bf16[2,384,384]{2,1,0:T(8,128)(2,1)S(1)}, u32[]{:S(2)}, u32[]{:S(2)}) collective-permute-start(bf16[2,384,384]{2,1,0:T(8,128)(2,1)S(1)} %get-tuple-element.41), channel_id=1, source_target_pairs={{0,252},{4,248},{8,244},{12,240},{16,236},{20,232},{24,228},{28,22... | collective-permute-start | bytes 1769480 | tf_op jit(solution)/shard_map/ppermute | solution.py:122
  19.6 0.1 collective-permute-start.9
  19.7 5.6 %collective-permute-start.3 = (bf16[1,384,384]{2,1,0:T(8,128)(2,1)}, bf16[1,384,384]{2,1,0:T(8,128)(2,1)S(1)}, u32[]{:S(2)}, u32[]{:S(2)}) collective-permute-start(bf16[1,384,384]{2,1,0:T(8,128)(2,1)} %get-tuple-element.39), channel_id=1, source_target_pairs={{0,252},{4,248},{8,244},{12,240},{16,236},{20,232},{24,228},{28,22... | collective-permute-start | bytes 884744 | tf_op jit(solution)/shard_map/ppermute | solution.py:122
  25.3 0.5 iota_add_fusion
  26.0 8.4 %convert_bitcast_fusion.1 = bf16[8,768,384]{1,2,0:T(8,128)(2,1)S(1)} fusion(bf16[1,8,768,768]{3,2,1,0:T(8,128)(2,1)} %param.8, bf16[8,768,384]{2,1,0:T(8,128)(2,1)} %param.5, pred[8,768]{1,0:T(8,128)(4,1)S(1)} %iota_compare_fusion.7), kind=kOutput, calls=%fused_computation.4 | convolution fusion | flops 3628597248 | bytes 18880512 | tf_op jit(solution)/shard_map/sab,sbc->sac/dot_general | solution.py:151
  34.5 5.8 %convert_bitcast_fusion.half_ref = bf16[8,768,384]{2,1,0:T(8,128)(2,1)} fusion(bf16[8,768,384]{1,2,0:T(8,128)(2,1)S(1)} %convert_bitcast_fusion.1, s32[768]{0:T(1024)S(1)} %fusion.40), kind=kOutput, calls=%fused_computation.3 | convolution fusion | flops 3626827776 | bytes 9440256 | tf_op jit(solution)/shard_map/ia,sac->sic/dot_general | solution.py:157
  40.3 0.2 select_reduce_fusion
  40.5 22.6 %collective-permute-done.comp_ref = bf16[1,384,384]{2,1,0:T(8,128)(2,1)S(1)} collective-permute-done((bf16[1,384,384]{2,1,0:T(8,128)(2,1)}, bf16[1,384,384]{2,1,0:T(8,128)(2,1)S(1)}, u32[]{:S(2)}, u32[]{:S(2)}) %collective-permute-start) | collective-permute-done | bytes 294944 | tf_op jit(solution)/shard_map/ppermute | solution.py:122
  63.1 0.7 copy-done.10
  63.8 2.5 %terms.5 = (f32[1,384,384]{2,1,0:T(8,128)}, bf16[1,384,384]{2,1,0:T(8,128)(2,1)}) custom-call(bf16[8,768,384]{2,1,0:T(8,128)(2,1)} %convert_bitcast_fusion.half_ref, bf16[1,384,384]{2,1,0:T(8,128)(2,1)} %copy-done.10), custom_call_target="tpu_custom_call" | custom-call | tf_op jit(solution)/shard_map/terms/pallas_call | solution.py:81
  66.4 41.0 %collective-permute-done.3.comp_ref = bf16[1,384,384]{2,1,0:T(8,128)(2,1)S(1)} collective-permute-done((bf16[1,384,384]{2,1,0:T(8,128)(2,1)}, bf16[1,384,384]{2,1,0:T(8,128)(2,1)S(1)}, u32[]{:S(2)}, u32[]{:S(2)}) %collective-permute-start.3) | collective-permute-done | bytes 294944 | tf_op jit(solution)/shard_map/ppermute | solution.py:122
  107.4 0.7 copy-done.11
  108.1 2.5 %terms.6 = (f32[1,384,384]{2,1,0:T(8,128)}, bf16[1,384,384]{2,1,0:T(8,128)(2,1)}) custom-call(bf16[8,768,384]{2,1,0:T(8,128)(2,1)} %convert_bitcast_fusion.half_ref, bf16[1,384,384]{2,1,0:T(8,128)(2,1)} %copy-done.11), custom_call_target="tpu_custom_call" | custom-call | tf_op jit(solution)/shard_map/terms/pallas_call | solution.py:81
  110.6 2.7 %fusion.13.half_ref = bf16[1,768,384]{2,1,0:T(8,128)(2,1)} fusion(s32[768]{0:T(1024)S(1)} %fusion.51, bf16[8,768,384]{1,2,0:T(8,128)(2,1)} %copy-done.18), kind=kOutput, calls=%fused_computation.16 | convolution fusion | flops 453869568 | bytes 1182720 | tf_op jit(solution)/shard_map/ia,sac->sic/dot_general | solution.py:157
  113.3 5.1 %collective-permute-start.21 = (bf16[1,384,384]{2,1,0:T(8,128)(2,1)S(1)}, bf16[1,384,384]{2,1,0:T(8,128)(2,1)S(1)}, u32[]{:S(2)}, u32[]{:S(2)}) collective-permute-start(bf16[1,384,384]{2,1,0:T(8,128)(2,1)S(1)} %get-tuple-element.37), channel_id=1, source_target_pairs={{0,252},{4,248},{8,244},{12,240},{16,236},{20,232},{24,228},{28,22... | collective-permute-start | bytes 884744 | tf_op jit(solution)/shard_map/ppermute | solution.py:122
  118.4 3.1 %terms.7 = (f32[2,384,384]{2,1,0:T(8,128)}, bf16[2,384,384]{2,1,0:T(8,128)(2,1)}) custom-call(bf16[8,768,384]{2,1,0:T(8,128)(2,1)} %convert_bitcast_fusion.half_ref, bf16[2,384,384]{2,1,0:T(8,128)(2,1)} %copy-done.6), custom_call_target="tpu_custom_call" | custom-call | tf_op jit(solution)/shard_map/terms/pallas_call | solution.py:81
  121.5 0.8 copy-done.5
  122.3 3.1 %terms.8 = (f32[2,384,384]{2,1,0:T(8,128)}, bf16[2,384,384]{2,1,0:T(8,128)(2,1)}) custom-call(bf16[8,768,384]{2,1,0:T(8,128)(2,1)} %convert_bitcast_fusion.half_ref, bf16[2,384,384]{2,1,0:T(8,128)(2,1)} %copy-done.5), custom_call_target="tpu_custom_call" | custom-call | tf_op jit(solution)/shard_map/terms/pallas_call | solution.py:81
  125.5 0.7 copy-done.12
  126.2 2.5 %terms.9 = (f32[1,384,384]{2,1,0:T(8,128)}, bf16[1,384,384]{2,1,0:T(8,128)(2,1)}) custom-call(bf16[1,768,384]{2,1,0:T(8,128)(2,1)} %fusion.13.half_ref, bf16[1,384,384]{2,1,0:T(8,128)(2,1)} %copy-done.12), custom_call_target="tpu_custom_call" | custom-call | tf_op jit(solution)/shard_map/terms/pallas_call | solution.py:81
  128.7 1.0 convert_add_fusion.5
  129.7 1.5 collective-permute-start.2
  131.4 0.1 collective-permute-start.5
  131.5 7.3 %collective-permute-done.2 = bf16[1,192,384]{2,1,0:T(8,128)(2,1)S(1)} collective-permute-done((bf16[1,192,384]{2,1,0:T(8,128)(2,1)S(1)}, bf16[1,192,384]{2,1,0:T(8,128)(2,1)S(1)}, u32[]{:S(2)}, u32[]{:S(2)}) %collective-permute-start.2) | collective-permute-done | bytes 147488 | tf_op jit(solution)/shard_map/ppermute | solution.py:122
  138.9 3.1 %collective-permute-done.5 = bf16[1,192,384]{2,1,0:T(8,128)(2,1)S(1)} collective-permute-done((bf16[1,192,384]{2,1,0:T(8,128)(2,1)S(1)}, bf16[1,192,384]{2,1,0:T(8,128)(2,1)S(1)}, u32[]{:S(2)}, u32[]{:S(2)}) %collective-permute-start.5) | collective-permute-done | bytes 147488 | tf_op jit(solution)/shard_map/ppermute | solution.py:122
  142.2 2.6 %collective-permute-start.7 = (bf16[2,48,384]{2,1,0:T(8,128)(2,1)S(1)}, bf16[2,48,384]{2,1,0:T(8,128)(2,1)S(1)}, u32[]{:S(2)}, u32[]{:S(2)}) collective-permute-start(bf16[2,48,384]{2,1,0:T(8,128)(2,1)S(1)} %get-tuple-element.50), channel_id=1, source_target_pairs={{0,192},{4,196},{8,200},{12,204},{16,208},{20,212},{24,216},{28,22... | collective-permute-start | bytes 221192 | tf_op jit(solution)/shard_map/ppermute | solution.py:122
  144.8 1.2 collective-permute-start.6
  146.1 0.7 copy-done.4
  146.8 2.2 part.2
  149.0 2.3 part.3
  151.3 1.4 collective-permute-start.13
  152.7 0.1 collective-permute-start.22
  153.0 1.4 collective-permute-start.20
  154.5 27.2 %collective-permute-done.22 = bf16[1,384,384]{2,1,0:T(8,128)(2,1)S(1)} collective-permute-done((bf16[1,384,384]{2,1,0:T(8,128)(2,1)}, bf16[1,384,384]{2,1,0:T(8,128)(2,1)S(1)}, u32[]{:S(2)}, u32[]{:S(2)}) %collective-permute-start.22) | collective-permute-done | bytes 294944 | tf_op jit(solution)/shard_map/ppermute | solution.py:122
  181.7 0.6 collective-permute-start.23
  182.4 2.4 %collective-permute-done.20 = bf16[1,192,384]{2,1,0:T(8,128)(2,1)S(1)} collective-permute-done((bf16[1,192,384]{2,1,0:T(8,128)(2,1)S(1)}, bf16[1,192,384]{2,1,0:T(8,128)(2,1)S(1)}, u32[]{:S(2)}, u32[]{:S(2)}) %collective-permute-start.20) | collective-permute-done | bytes 147488 | tf_op jit(solution)/shard_map/ppermute | solution.py:122
  184.8 1.3 collective-permute-done.23
  186.2 0.1 convert_add_fusion.1
  186.4 0.6 collective-permute-start.11
  187.0 0.4 copy-done.2
  187.5 0.6 collective-permute-start.14
  188.2 0.3 collective-permute-start.26
  188.5 2.5 %collective-permute-start.25 = (bf16[2,48,384]{2,1,0:T(8,128)(2,1)S(1)}, bf16[2,48,384]{2,1,0:T(8,128)(2,1)S(1)}, u32[]{:S(2)}, u32[]{:S(2)}) collective-permute-start(bf16[2,48,384]{2,1,0:T(8,128)(2,1)S(1)} %get-tuple-element.53), channel_id=1, source_target_pairs={{0,192},{4,196},{8,200},{12,204},{16,208},{20,212},{24,216},{28,22... | collective-permute-start | bytes 221192 | tf_op jit(solution)/shard_map/ppermute | solution.py:122
  191.0 1.2 collective-permute-start.24
  192.2 1.6 collective-permute-done.11
  193.8 3.0 %collective-permute-done.14 = bf16[2,192,384]{2,1,0:T(8,128)(2,1)S(1)} collective-permute-done((bf16[2,192,384]{2,1,0:T(8,128)(2,1)S(1)}, bf16[2,192,384]{2,1,0:T(8,128)(2,1)S(1)}, u32[]{:S(2)}, u32[]{:S(2)}) %collective-permute-start.14) | collective-permute-done | bytes 294944 | tf_op jit(solution)/shard_map/ppermute | solution.py:122
  197.0 0.5 collective-permute-start.17
  197.5 2.5 %collective-permute-start.16 = (bf16[4,48,384]{2,1,0:T(8,128)(2,1)S(1)}, bf16[4,48,384]{2,1,0:T(8,128)(2,1)S(1)}, u32[]{:S(2)}, u32[]{:S(2)}) collective-permute-start(bf16[4,48,384]{2,1,0:T(8,128)(2,1)S(1)} %get-tuple-element.44), channel_id=1, source_target_pairs={{0,192},{4,196},{8,200},{12,204},{16,208},{20,212},{24,216},{28,22... | collective-permute-start | bytes 442376 | tf_op jit(solution)/shard_map/ppermute | solution.py:122
  199.9 1.2 collective-permute-start.15
  201.2 3.4 %collective-permute-done.17 = bf16[4,48,384]{2,1,0:T(8,128)(2,1)S(1)} collective-permute-done((bf16[4,48,384]{2,1,0:T(8,128)(2,1)S(1)}, bf16[4,48,384]{2,1,0:T(8,128)(2,1)S(1)}, u32[]{:S(2)}, u32[]{:S(2)}) %collective-permute-start.17) | collective-permute-done | bytes 147488 | tf_op jit(solution)/shard_map/ppermute | solution.py:122
  204.6 1.3 collective-permute-done.16
  206.2 4.4 %collective-permute-start.28 = (bf16[8,12,384]{2,1,0:T(8,128)(2,1)S(1)}, bf16[8,12,384]{2,1,0:T(8,128)(2,1)S(1)}, u32[]{:S(2)}, u32[]{:S(2)}) collective-permute-start(bf16[8,12,384]{2,1,0:T(8,128)(2,1)S(1)} %get-tuple-element.47), channel_id=1, source_target_pairs={{0,32},{4,36},{8,40},{12,44},{16,48},{20,52},{24,56},{28,60},{32,0... | collective-permute-start | bytes 221192 | tf_op jit(solution)/shard_map/ppermute | solution.py:122
  210.6 1.3 collective-permute-start.27
  211.9 0.2 collective-permute-done.29
  212.1 2.4 %collective-permute-done.28 = bf16[8,12,384]{2,1,0:T(8,128)(2,1)S(1)} collective-permute-done((bf16[8,12,384]{2,1,0:T(8,128)(2,1)S(1)}, bf16[8,12,384]{2,1,0:T(8,128)(2,1)S(1)}, u32[]{:S(2)}, u32[]{:S(2)}) %collective-permute-start.28) | collective-permute-done | bytes 73760 | tf_op jit(solution)/shard_map/ppermute | solution.py:122
  214.5 3.0 %collective-permute-done.27 = bf16[8,12,384]{2,1,0:T(8,128)(2,1)S(1)} collective-permute-done((bf16[8,12,384]{2,1,0:T(8,128)(2,1)S(1)}, bf16[8,12,384]{2,1,0:T(8,128)(2,1)S(1)}, u32[]{:S(2)}, u32[]{:S(2)}) %collective-permute-start.27) | collective-permute-done | bytes 73760 | tf_op jit(solution)/shard_map/ppermute | solution.py:122
  217.6 15.9 %all_gather.3 = bf16[32,12,384]{2,0,1:T(8,128)(2,1)S(1)} all-gather(bf16[8,12,384]{2,0,1:T(8,128)(2,1)S(1)} %copy.23), channel_id=1, replica_groups=mesh['pair'=64,'sec'=4] {'sec'}, dimensions={0}, use_global_device_ids=true | all-gather | bytes 368640 | tf_op jit(solution)/shard_map/all_gather | solution.py:192
  233.5 0.1 copy.24
  233.6 0.6 gather_fusion
  234.2 0.6 copy.25
  (94 shorter events, 2.0 us)
Async XLA Ops:
  0.0 13.7 %copy-start = (bf16[1,8,384,384]{3,2,1,0:T(8,128)(2,1)S(1)}, bf16[1,8,384,384]{3,2,1,0:T(8,128)(2,1)}, u32[]{:S(2)}) copy-start(bf16[1,8,384,384]{3,2,1,0:T(8,128)(2,1)} %param.9) | copy-start | bytes 7077892
  0.0 25.8 %copy-start.15 = (s32[32]{0:T(128)S(1)}, s32[32]{0:T(128)}, u32[]{:S(2)}) copy-start(s32[32]{0:T(128)} %param.6) | copy-start | bytes 388
  1.9 61.2 %collective-permute-start = (bf16[1,384,384]{2,1,0:T(8,128)(2,1)}, bf16[1,384,384]{2,1,0:T(8,128)(2,1)S(1)}, u32[]{:S(2)}, u32[]{:S(2)}) collective-permute-start(bf16[1,384,384]{2,1,0:T(8,128)(2,1)} %slice_bitcast_fusion.2), channel_id=1, source_target_pairs={{0,252},{4,248},{8,244},{12,240},{16,236},{20,232},{24,228},{28,22... | collective-permute-start | bytes 884744 | tf_op jit(solution)/shard_map/ppermute | solution.py:122
  13.7 111.7 %collective-permute-start.18 = (bf16[1,384,384]{2,1,0:T(8,128)(2,1)}, bf16[1,384,384]{2,1,0:T(8,128)(2,1)S(1)}, u32[]{:S(2)}, u32[]{:S(2)}) collective-permute-start(bf16[1,384,384]{2,1,0:T(8,128)(2,1)} %get-tuple-element.38), channel_id=1, source_target_pairs={{0,252},{4,248},{8,244},{12,240},{16,236},{20,232},{24,228},{28,22... | collective-permute-start | bytes 884744 | tf_op jit(solution)/shard_map/ppermute | solution.py:122
  13.8 107.6 %collective-permute-start.12 = (bf16[2,384,384]{2,1,0:T(8,128)(2,1)S(1)}, bf16[2,384,384]{2,1,0:T(8,128)(2,1)S(1)}, u32[]{:S(2)}, u32[]{:S(2)}) collective-permute-start(bf16[2,384,384]{2,1,0:T(8,128)(2,1)S(1)} %get-tuple-element.41), channel_id=1, source_target_pairs={{0,252},{4,248},{8,244},{12,240},{16,236},{20,232},{24,228},{28,22... | collective-permute-start | bytes 1769480 | tf_op jit(solution)/shard_map/ppermute | solution.py:122
  19.6 93.6 %collective-permute-start.9 = (bf16[2,384,384]{2,1,0:T(8,128)(2,1)S(1)}, bf16[2,384,384]{2,1,0:T(8,128)(2,1)S(1)}, u32[]{:S(2)}, u32[]{:S(2)}) collective-permute-start(bf16[2,384,384]{2,1,0:T(8,128)(2,1)S(1)} %get-tuple-element.40), channel_id=1, source_target_pairs={{0,252},{4,248},{8,244},{12,240},{16,236},{20,232},{24,228},{28,22... | collective-permute-start | bytes 1769480 | tf_op jit(solution)/shard_map/ppermute | solution.py:122
  19.7 87.6 %collective-permute-start.3 = (bf16[1,384,384]{2,1,0:T(8,128)(2,1)}, bf16[1,384,384]{2,1,0:T(8,128)(2,1)S(1)}, u32[]{:S(2)}, u32[]{:S(2)}) collective-permute-start(bf16[1,384,384]{2,1,0:T(8,128)(2,1)} %get-tuple-element.39), channel_id=1, source_target_pairs={{0,252},{4,248},{8,244},{12,240},{16,236},{20,232},{24,228},{28,22... | collective-permute-start | bytes 884744 | tf_op jit(solution)/shard_map/ppermute | solution.py:122
  34.4 5.8 %copy-start.18 = (bf16[8,768,384]{1,2,0:T(8,128)(2,1)}, bf16[8,768,384]{1,2,0:T(8,128)(2,1)S(1)}, u32[]{:S(2)}) copy-start(bf16[8,768,384]{1,2,0:T(8,128)(2,1)S(1)} %convert_bitcast_fusion.1) | copy-start | bytes 14155780
  34.5 5.8 %copy-start.16 = (s32[32]{0:T(128)S(1)}, s32[32]{0:T(128)}, u32[]{:S(2)}) copy-start(s32[32]{0:T(128)} %param.7) | copy-start | bytes 388
  34.5 5.8 %copy-start.17 = (s32[8]{0:T(128)S(1)}, s32[8]{0:T(128)}, u32[]{:S(2)}) copy-start(s32[8]{0:T(128)} %iota_add_fusion) | copy-start | bytes 100
  63.1 0.7 copy-start.10
  66.4 62.3 %collective-permute-start.1 = (bf16[1,384,384]{2,1,0:T(8,128)(2,1)}, bf16[1,384,384]{2,1,0:T(8,128)(2,1)}, u32[]{:S(2)}, u32[]{:S(2)}) collective-permute-start(bf16[1,384,384]{2,1,0:T(8,128)(2,1)} %get-tuple-element.22), channel_id=1, source_target_pairs={{0,64},{4,68},{8,72},{12,76},{16,80},{20,84},{24,88},{28,92},{32,9... | collective-permute-start | bytes 884744 | tf_op jit(solution)/shard_map/ppermute | solution.py:122
  107.4 0.7 copy-start.11
  110.6 20.7 %collective-permute-start.4 = (bf16[1,384,384]{2,1,0:T(8,128)(2,1)}, bf16[1,384,384]{2,1,0:T(8,128)(2,1)S(1)}, u32[]{:S(2)}, u32[]{:S(2)}) collective-permute-start(bf16[1,384,384]{2,1,0:T(8,128)(2,1)} %get-tuple-element.26), channel_id=1, source_target_pairs={{0,64},{4,68},{8,72},{12,76},{16,80},{20,84},{24,88},{28,92},{32,9... | collective-permute-start | bytes 884744 | tf_op jit(solution)/shard_map/ppermute | solution.py:122
  113.2 5.1 %copy-start.6 = (bf16[2,384,384]{2,1,0:T(8,128)(2,1)}, bf16[2,384,384]{2,1,0:T(8,128)(2,1)S(1)}, u32[]{:S(2)}) copy-start(bf16[2,384,384]{2,1,0:T(8,128)(2,1)S(1)} %collective-permute-done.9.comp_ref) | copy-start | bytes 1769476
  113.3 32.8 %collective-permute-start.21 = (bf16[1,384,384]{2,1,0:T(8,128)(2,1)S(1)}, bf16[1,384,384]{2,1,0:T(8,128)(2,1)S(1)}, u32[]{:S(2)}, u32[]{:S(2)}) collective-permute-start(bf16[1,384,384]{2,1,0:T(8,128)(2,1)S(1)} %get-tuple-element.37), channel_id=1, source_target_pairs={{0,252},{4,248},{8,244},{12,240},{16,236},{20,232},{24,228},{28,22... | collective-permute-start | bytes 884744 | tf_op jit(solution)/shard_map/ppermute | solution.py:122
  121.5 0.8 copy-start.5
  122.3 6.4 %copy-start.8 = (f32[1,384,384]{2,1,0:T(8,128)S(1)}, f32[1,384,384]{2,1,0:T(8,128)}, u32[]{:S(2)}) copy-start(f32[1,384,384]{2,1,0:T(8,128)} %get-tuple-element.21) | copy-start | bytes 1769476
  125.4 5.9 %copy-start.9 = (f32[1,384,384]{2,1,0:T(8,128)S(1)}, f32[1,384,384]{2,1,0:T(8,128)}, u32[]{:S(2)}) copy-start(f32[1,384,384]{2,1,0:T(8,128)} %get-tuple-element.25) | copy-start | bytes 1769476
  125.4 0.7 copy-start.12
  128.7 24.2 %collective-permute-start.19 = (bf16[1,384,384]{2,1,0:T(8,128)(2,1)}, bf16[1,384,384]{2,1,0:T(8,128)(2,1)S(1)}, u32[]{:S(2)}, u32[]{:S(2)}) collective-permute-start(bf16[1,384,384]{2,1,0:T(8,128)(2,1)} %get-tuple-element.35), channel_id=1, source_target_pairs={{0,8},{4,12},{8,0},{12,4},{16,24},{20,28},{24,16},{28,20},{32,40},... | collective-permute-start | bytes 884744 | tf_op jit(solution)/shard_map/ppermute | solution.py:122
  129.7 9.1 %collective-permute-start.2 = (bf16[1,192,384]{2,1,0:T(8,128)(2,1)S(1)}, bf16[1,192,384]{2,1,0:T(8,128)(2,1)S(1)}, u32[]{:S(2)}, u32[]{:S(2)}) collective-permute-start(bf16[1,192,384]{2,1,0:T(8,128)(2,1)S(1)} %slice.239), channel_id=1, source_target_pairs={{0,8},{4,12},{8,0},{12,4},{16,24},{20,28},{24,16},{28,20},{32,40},... | collective-permute-start | bytes 442376 | tf_op jit(solution)/shard_map/ppermute | solution.py:122
  131.4 10.6 %collective-permute-start.5 = (bf16[1,192,384]{2,1,0:T(8,128)(2,1)S(1)}, bf16[1,192,384]{2,1,0:T(8,128)(2,1)S(1)}, u32[]{:S(2)}, u32[]{:S(2)}) collective-permute-start(bf16[1,192,384]{2,1,0:T(8,128)(2,1)S(1)} %slice.238), channel_id=1, source_target_pairs={{0,8},{4,12},{8,0},{12,4},{16,24},{20,28},{24,16},{28,20},{32,40},... | collective-permute-start | bytes 442376 | tf_op jit(solution)/shard_map/ppermute | solution.py:122
  142.1 9.2 %collective-permute-start.8 = (bf16[2,48,384]{2,1,0:T(8,128)(2,1)S(1)}, bf16[2,48,384]{2,1,0:T(8,128)(2,1)S(1)}, u32[]{:S(2)}, u32[]{:S(2)}) collective-permute-start(bf16[2,48,384]{2,1,0:T(8,128)(2,1)S(1)} %get-tuple-element.49), channel_id=1, source_target_pairs={{0,196},{4,192},{8,204},{12,200},{16,212},{20,208},{24,220},{28,21... | collective-permute-start | bytes 221192 | tf_op jit(solution)/shard_map/ppermute | solution.py:122
  142.2 10.5 %collective-permute-start.7 = (bf16[2,48,384]{2,1,0:T(8,128)(2,1)S(1)}, bf16[2,48,384]{2,1,0:T(8,128)(2,1)S(1)}, u32[]{:S(2)}, u32[]{:S(2)}) collective-permute-start(bf16[2,48,384]{2,1,0:T(8,128)(2,1)S(1)} %get-tuple-element.50), channel_id=1, source_target_pairs={{0,192},{4,196},{8,200},{12,204},{16,208},{20,212},{24,216},{28,22... | collective-permute-start | bytes 221192 | tf_op jit(solution)/shard_map/ppermute | solution.py:122
  144.8 8.0 %collective-permute-start.6 = (bf16[2,48,384]{2,1,0:T(8,128)(2,1)S(1)}, bf16[2,48,384]{2,1,0:T(8,128)(2,1)S(1)}, u32[]{:S(2)}, u32[]{:S(2)}) collective-permute-start(bf16[2,48,384]{2,1,0:T(8,128)(2,1)S(1)} %get-tuple-element.48), channel_id=1, source_target_pairs={{0,4},{4,0},{8,12},{12,8},{16,20},{20,16},{24,28},{28,24},{32,36},... | collective-permute-start | bytes 221192 | tf_op jit(solution)/shard_map/ppermute | solution.py:122
  146.1 0.7 copy-start.4
  149.0 2.3 copy-start.14
  149.0 2.3 copy-start.13
  149.0 3.9 %copy-start.7 = (f32[1,384,384]{2,1,0:T(8,128)S(1)}, f32[1,384,384]{2,1,0:T(8,128)}, u32[]{:S(2)}) copy-start(f32[1,384,384]{2,1,0:T(8,128)} %get-tuple-element.34) | copy-start | bytes 1769476
  151.3 30.4 %copy-start.1 = (f32[1,384,384]{2,1,0:T(8,128)S(1)}, f32[1,384,384]{2,1,0:T(8,128)}, u32[]{:S(2)}) copy-start(f32[1,384,384]{2,1,0:T(8,128)} %part.2) | copy-start | bytes 1769476
  151.3 34.9 %collective-permute-start.10 = (bf16[2,384,384]{2,1,0:T(8,128)(2,1)S(1)}, bf16[2,384,384]{2,1,0:T(8,128)(2,1)S(1)}, u32[]{:S(2)}, u32[]{:S(2)}) collective-permute-start(bf16[2,384,384]{2,1,0:T(8,128)(2,1)S(1)} %copy-done.14), channel_id=1, source_target_pairs={{0,64},{4,68},{8,72},{12,76},{16,80},{20,84},{24,88},{28,92},{32,9... | collective-permute-start | bytes 1769480 | tf_op jit(solution)/shard_map/ppermute | solution.py:122
  151.3 35.7 %collective-permute-start.13 = (bf16[2,384,384]{2,1,0:T(8,128)(2,1)S(1)}, bf16[2,384,384]{2,1,0:T(8,128)(2,1)S(1)}, u32[]{:S(2)}, u32[]{:S(2)}) collective-permute-start(bf16[2,384,384]{2,1,0:T(8,128)(2,1)S(1)} %copy-done.13), channel_id=1, source_target_pairs={{0,64},{4,68},{8,72},{12,76},{16,80},{20,84},{24,88},{28,92},{32,9... | collective-permute-start | bytes 1769480 | tf_op jit(solution)/shard_map/ppermute | solution.py:122
  152.7 28.9 %collective-permute-start.22 = (bf16[1,384,384]{2,1,0:T(8,128)(2,1)}, bf16[1,384,384]{2,1,0:T(8,128)(2,1)S(1)}, u32[]{:S(2)}, u32[]{:S(2)}) collective-permute-start(bf16[1,384,384]{2,1,0:T(8,128)(2,1)} %part.3), channel_id=1, source_target_pairs={{0,64},{4,68},{8,72},{12,76},{16,80},{20,84},{24,88},{28,92},{32,9... | collective-permute-start | bytes 884744 | tf_op jit(solution)/shard_map/ppermute | solution.py:122
  153.0 33.2 %copy-start.3 = (f32[2,384,384]{2,1,0:T(8,128)S(1)}, f32[2,384,384]{2,1,0:T(8,128)}, u32[]{:S(2)}) copy-start(f32[2,384,384]{2,1,0:T(8,128)} %get-tuple-element.28) | copy-start | bytes 3538948
  153.0 31.8 %collective-permute-start.20 = (bf16[1,192,384]{2,1,0:T(8,128)(2,1)S(1)}, bf16[1,192,384]{2,1,0:T(8,128)(2,1)S(1)}, u32[]{:S(2)}, u32[]{:S(2)}) collective-permute-start(bf16[1,192,384]{2,1,0:T(8,128)(2,1)S(1)} %slice.237), channel_id=1, source_target_pairs={{0,64},{4,68},{8,72},{12,76},{16,80},{20,84},{24,88},{28,92},{32,9... | collective-permute-start | bytes 442376 | tf_op jit(solution)/shard_map/ppermute | solution.py:122
  181.7 4.4 %collective-permute-start.23 = (bf16[1,192,384]{2,1,0:T(8,128)(2,1)S(1)}, bf16[1,192,384]{2,1,0:T(8,128)(2,1)S(1)}, u32[]{:S(2)}, u32[]{:S(2)}) collective-permute-start(bf16[1,192,384]{2,1,0:T(8,128)(2,1)S(1)} %slice.236), channel_id=1, source_target_pairs={{0,8},{4,12},{8,0},{12,4},{16,24},{20,28},{24,16},{28,20},{32,40},... | collective-permute-start | bytes 442376 | tf_op jit(solution)/shard_map/ppermute | solution.py:122
  186.1 1.3 copy-start.2
  186.4 7.4 %collective-permute-start.11 = (bf16[2,192,384]{2,1,0:T(8,128)(2,1)S(1)}, bf16[2,192,384]{2,1,0:T(8,128)(2,1)S(1)}, u32[]{:S(2)}, u32[]{:S(2)}) collective-permute-start(bf16[2,192,384]{2,1,0:T(8,128)(2,1)S(1)} %slice.235), channel_id=1, source_target_pairs={{0,8},{4,12},{8,0},{12,4},{16,24},{20,28},{24,16},{28,20},{32,40},... | collective-permute-start | bytes 884744 | tf_op jit(solution)/shard_map/ppermute | solution.py:122
  187.5 9.2 %collective-permute-start.14 = (bf16[2,192,384]{2,1,0:T(8,128)(2,1)S(1)}, bf16[2,192,384]{2,1,0:T(8,128)(2,1)S(1)}, u32[]{:S(2)}, u32[]{:S(2)}) collective-permute-start(bf16[2,192,384]{2,1,0:T(8,128)(2,1)S(1)} %slice.234), channel_id=1, source_target_pairs={{0,8},{4,12},{8,0},{12,4},{16,24},{20,28},{24,16},{28,20},{32,40},... | collective-permute-start | bytes 884744 | tf_op jit(solution)/shard_map/ppermute | solution.py:122
  188.2 11.7 %collective-permute-start.26 = (bf16[2,48,384]{2,1,0:T(8,128)(2,1)S(1)}, bf16[2,48,384]{2,1,0:T(8,128)(2,1)S(1)}, u32[]{:S(2)}, u32[]{:S(2)}) collective-permute-start(bf16[2,48,384]{2,1,0:T(8,128)(2,1)S(1)} %get-tuple-element.52), channel_id=1, source_target_pairs={{0,196},{4,192},{8,204},{12,200},{16,212},{20,208},{24,220},{28,21... | collective-permute-start | bytes 221192 | tf_op jit(solution)/shard_map/ppermute | solution.py:122
  188.5 12.6 %collective-permute-start.25 = (bf16[2,48,384]{2,1,0:T(8,128)(2,1)S(1)}, bf16[2,48,384]{2,1,0:T(8,128)(2,1)S(1)}, u32[]{:S(2)}, u32[]{:S(2)}) collective-permute-start(bf16[2,48,384]{2,1,0:T(8,128)(2,1)S(1)} %get-tuple-element.53), channel_id=1, source_target_pairs={{0,192},{4,196},{8,200},{12,204},{16,208},{20,212},{24,216},{28,22... | collective-permute-start | bytes 221192 | tf_op jit(solution)/shard_map/ppermute | solution.py:122
  191.0 10.2 %collective-permute-start.24 = (bf16[2,48,384]{2,1,0:T(8,128)(2,1)S(1)}, bf16[2,48,384]{2,1,0:T(8,128)(2,1)S(1)}, u32[]{:S(2)}, u32[]{:S(2)}) collective-permute-start(bf16[2,48,384]{2,1,0:T(8,128)(2,1)S(1)} %get-tuple-element.51), channel_id=1, source_target_pairs={{0,4},{4,0},{8,12},{12,8},{16,20},{20,16},{24,28},{28,24},{32,36},... | collective-permute-start | bytes 221192 | tf_op jit(solution)/shard_map/ppermute | solution.py:122
  197.0 7.7 %collective-permute-start.17 = (bf16[4,48,384]{2,1,0:T(8,128)(2,1)S(1)}, bf16[4,48,384]{2,1,0:T(8,128)(2,1)S(1)}, u32[]{:S(2)}, u32[]{:S(2)}) collective-permute-start(bf16[4,48,384]{2,1,0:T(8,128)(2,1)S(1)} %get-tuple-element.43), channel_id=1, source_target_pairs={{0,196},{4,192},{8,204},{12,200},{16,212},{20,208},{24,220},{28,21... | collective-permute-start | bytes 442376 | tf_op jit(solution)/shard_map/ppermute | solution.py:122
  197.5 8.4 %collective-permute-start.16 = (bf16[4,48,384]{2,1,0:T(8,128)(2,1)S(1)}, bf16[4,48,384]{2,1,0:T(8,128)(2,1)S(1)}, u32[]{:S(2)}, u32[]{:S(2)}) collective-permute-start(bf16[4,48,384]{2,1,0:T(8,128)(2,1)S(1)} %get-tuple-element.44), channel_id=1, source_target_pairs={{0,192},{4,196},{8,200},{12,204},{16,208},{20,212},{24,216},{28,22... | collective-permute-start | bytes 442376 | tf_op jit(solution)/shard_map/ppermute | solution.py:122
  199.9 6.0 %collective-permute-start.15 = (bf16[4,48,384]{2,1,0:T(8,128)(2,1)S(1)}, bf16[4,48,384]{2,1,0:T(8,128)(2,1)S(1)}, u32[]{:S(2)}, u32[]{:S(2)}) collective-permute-start(bf16[4,48,384]{2,1,0:T(8,128)(2,1)S(1)} %get-tuple-element.42), channel_id=1, source_target_pairs={{0,4},{4,0},{8,12},{12,8},{16,20},{20,16},{24,28},{28,24},{32,36},... | collective-permute-start | bytes 442376 | tf_op jit(solution)/shard_map/ppermute | solution.py:122
  206.1 6.0 %collective-permute-start.29 = (bf16[8,12,384]{2,1,0:T(8,128)(2,1)S(1)}, bf16[8,12,384]{2,1,0:T(8,128)(2,1)S(1)}, u32[]{:S(2)}, u32[]{:S(2)}) collective-permute-start(bf16[8,12,384]{2,1,0:T(8,128)(2,1)S(1)} %get-tuple-element.46), channel_id=1, source_target_pairs={{0,48},{4,52},{8,56},{12,60},{16,32},{20,36},{24,40},{28,44},{32,1... | collective-permute-start | bytes 221192 | tf_op jit(solution)/shard_map/ppermute | solution.py:122
  206.2 8.3 %collective-permute-start.28 = (bf16[8,12,384]{2,1,0:T(8,128)(2,1)S(1)}, bf16[8,12,384]{2,1,0:T(8,128)(2,1)S(1)}, u32[]{:S(2)}, u32[]{:S(2)}) collective-permute-start(bf16[8,12,384]{2,1,0:T(8,128)(2,1)S(1)} %get-tuple-element.47), channel_id=1, source_target_pairs={{0,32},{4,36},{8,40},{12,44},{16,48},{20,52},{24,56},{28,60},{32,0... | collective-permute-start | bytes 221192 | tf_op jit(solution)/shard_map/ppermute | solution.py:122
  210.6 6.9 %collective-permute-start.27 = (bf16[8,12,384]{2,1,0:T(8,128)(2,1)S(1)}, bf16[8,12,384]{2,1,0:T(8,128)(2,1)S(1)}, u32[]{:S(2)}, u32[]{:S(2)}) collective-permute-start(bf16[8,12,384]{2,1,0:T(8,128)(2,1)S(1)} %get-tuple-element.45), channel_id=1, source_target_pairs={{0,16},{4,20},{8,24},{12,28},{16,0},{20,4},{24,8},{28,12},{32,48},... | collective-permute-start | bytes 221192 | tf_op jit(solution)/shard_map/ppermute | solution.py:122

commit v3 on v2

--- a/solution.py
+++ b/solution.py
@@ -57,10 +57,8 @@
 
 
 def pick_sources(gathered, match, targets):
-    total = match.shape[0]
-    hits = match[None, :] == targets[:, None]
-    source = jnp.sum(jnp.where(hits, jnp.arange(total, dtype=jnp.int32)[None, :], 0), axis=1)
-    return gathered[source]
+    hits = (match[None, :] == targets[:, None]).astype(gathered.dtype)
+    return jnp.einsum("ts,sjc->tjc", hits, gathered, preferred_element_type=F32)
 
 
 def terms_kernel(half_ref, comp_ref, keep_ref, send_ref):
@@ -92,29 +90,6 @@
         ],
         interpret=INTERPRET,
         name="terms",
-    )(half, comp)
-
-
-def part_kernel(half_ref, comp_ref, out_ref):
-    out_ref[0] = lax.dot_general(
-        half_ref[0], comp_ref[0], (((1,), (1,)), ((), ())), preferred_element_type=F32
-    ).astype(out_ref.dtype)
-
-
-def part_of(half, comp, start, part, dtype):
-    sectors, cols, _ = comp.shape
-    rows = half.shape[1] // 2
-    return pl.pallas_call(
-        part_kernel,
-        grid=(sectors,),
-        in_specs=[
-            pl.BlockSpec((1, rows, cols), lambda s: (s + start, part, 0)),
-            pl.BlockSpec((1, cols, cols), lambda s: (s, 0, 0)),
-        ],
-        out_specs=pl.BlockSpec((1, rows, cols), lambda s: (s, 0, 0)),
-        out_shape=jax.ShapeDtypeStruct((sectors, rows, cols), dtype),
-        interpret=INTERPRET,
-        name="part",
     )(half, comp)
 
 
@@ -163,11 +138,7 @@
         if i:
             comp, _ = lax.optimization_barrier((comp, flows[-1][1]))
         source, start = routed[i in SWAPPED]
-        if i + 1 < len(CHUNKS):
-            flows.append(terms_of(source, comp, a - start))
-        else:
-            send = part_of(source, comp, a - start, 1, BF16)
-    flows.append((part_of(source, comp, a - start, 0, F32), send))
+        flows.append(terms_of(source, comp, a - start))
     def swap_four(perms, total):
         cut = total.shape[1] // 4
         got = [
@@ -193,7 +164,7 @@
     summed = pick_sources(gathered, match, targets)
     my_lines = pair * share + jnp.arange(share, dtype=jnp.int32)
     out_keep = my_lines[None, :] < rows_here[:, None]
-    return jnp.where(out_keep[:, :, None], summed, jnp.zeros_like(summed))
+    return jnp.where(out_keep[:, :, None], summed, jnp.zeros_like(summed)).astype(BF16)
 
 
 def solution(mesh):

time: 235 us -> 230 us (0.979)
    pallas_call x2 -> x0, Pallas kernels: 4.47 us -> none  [part_of(): pl.pallas_call(part_kernel, grid=(sectors,), in_specs=[pl.BlockSpec((1, r...]
    pallas_call x5 -> x6, Pallas kernels: 13.8 us -> 16.3 us  [terms_of(): pl.pallas_call(terms_kernel, grid=(sectors,), in_specs=[pl.BlockSpec((1,...]
  transfers between devices with their start and end apart: 30 -> 30, of which waited for: 14 -> 14; matrix products, arithmetic and copies ran while one was open for 9% -> 9% of each run, Pallas kernels for 8% -> 7%
where the time goes in v3:
time: 230 us; the launch traced here: 229 us
  waiting for transfers between devices  119 us (52%)
  starting transfers between devices  50.3 us (22%)
  matrix products  17.8 us (8%)
  Pallas kernels  16.3 us (7%)
  blocking collectives  15.9 us (7%)
  local copies, waits for them, and re-layouts  8.42 us (4%)
    ppermute x30, waiting for transfers between devices, exchange(): return lax.ppermute(value, 'pair', perm)  119 us
    ppermute x30, starting transfers between devices, exchange(): return lax.ppermute(value, 'pair', perm)  50.3 us
    pallas_call x6, Pallas kernels, terms_of(): pl.pallas_call(terms_kernel, grid=(sectors,), in_specs=[pl.BlockSpec((1,...  16.3 us
    all_gather x1, blocking collectives, product(): gathered = lax.all_gather(partial_rows, 'sec', axis=0, tiled=True)  15.9 us
    dot_general x2, matrix products, product(): jnp.einsum('ia,sac->sic', order, half[first:end], preferred_element_type=...  8.54 us
    dot_general x1, matrix products, product(): jnp.einsum('sab,sbc->sac', normal_ops[0], kept, preferred_element_type=F32)  8.39 us
  transfers between devices with their start and end apart: 30, of which 14 were waited for; matrix products, arithmetic and copies ran while one was open for 9% of the time, Pallas kernels for 7%

profile of v3, /device:TPU:1, one launch (start us, length us, event | category | flops | bytes accessed | tf_op | source)
XLA Modules:
  0.0 229.4 jit_solution(17311769421685843104)
XLA Ops:
  0.0 1.9 slice_bitcast_fusion.2
  1.9 9.8 %collective-permute-start = (bf16[1,384,384]{2,1,0:T(8,128)(2,1)}, bf16[1,384,384]{2,1,0:T(8,128)(2,1)S(1)}, u32[]{:S(2)}, u32[]{:S(2)}) collective-permute-start(bf16[1,384,384]{2,1,0:T(8,128)(2,1)} %slice_bitcast_fusion.2), channel_id=1, source_target_pairs={{0,252},{4,248},{8,244},{12,240},{16,236},{20,232},{24,228},{28,22... | collective-permute-start | bytes 884744 | tf_op jit(solution)/shard_map/ppermute | solution.py:97
  11.6 2.1 fusion.65
  13.7 0.1 fusion.66
  13.8 5.8 %collective-permute-start.12 = (bf16[2,384,384]{2,1,0:T(8,128)(2,1)S(1)}, bf16[2,384,384]{2,1,0:T(8,128)(2,1)S(1)}, u32[]{:S(2)}, u32[]{:S(2)}) collective-permute-start(bf16[2,384,384]{2,1,0:T(8,128)(2,1)S(1)} %get-tuple-element.45), channel_id=1, source_target_pairs={{0,252},{4,248},{8,244},{12,240},{16,236},{20,232},{24,228},{28,22... | collective-permute-start | bytes 1769480 | tf_op jit(solution)/shard_map/ppermute | solution.py:97
  19.6 0.1 collective-permute-start.9
  19.7 5.6 %collective-permute-start.3 = (bf16[1,384,384]{2,1,0:T(8,128)(2,1)}, bf16[1,384,384]{2,1,0:T(8,128)(2,1)S(1)}, u32[]{:S(2)}, u32[]{:S(2)}) collective-permute-start(bf16[1,384,384]{2,1,0:T(8,128)(2,1)} %get-tuple-element.43), channel_id=1, source_target_pairs={{0,252},{4,248},{8,244},{12,240},{16,236},{20,232},{24,228},{28,22... | collective-permute-start | bytes 884744 | tf_op jit(solution)/shard_map/ppermute | solution.py:97
  25.4 0.1 iota_compare_fusion.7
  25.4 8.4 %convert_bitcast_fusion.1 = bf16[8,768,384]{1,2,0:T(8,128)(2,1)S(1)} fusion(bf16[1,8,768,768]{3,2,1,0:T(8,128)(2,1)} %param.8, bf16[8,768,384]{2,1,0:T(8,128)(2,1)} %param.5, pred[8,768]{1,0:T(8,128)(4,1)S(1)} %iota_compare_fusion.7), kind=kOutput, calls=%fused_computation.3 | convolution fusion | flops 3628597248 | bytes 18880512 | tf_op jit(solution)/shard_map/sab,sbc->sac/dot_general | solution.py:126
  33.9 5.9 %convert_bitcast_fusion.half_ref = bf16[8,768,384]{2,1,0:T(8,128)(2,1)} fusion(bf16[8,768,384]{1,2,0:T(8,128)(2,1)S(1)} %convert_bitcast_fusion.1, s32[768]{0:T(1024)S(1)} %fusion.41), kind=kOutput, calls=%fused_computation.2 | convolution fusion | flops 3626827776 | bytes 9440256 | tf_op jit(solution)/shard_map/ia,sac->sic/dot_general | solution.py:132
  39.8 23.3 %collective-permute-done.comp_ref = bf16[1,384,384]{2,1,0:T(8,128)(2,1)S(1)} collective-permute-done((bf16[1,384,384]{2,1,0:T(8,128)(2,1)}, bf16[1,384,384]{2,1,0:T(8,128)(2,1)S(1)}, u32[]{:S(2)}, u32[]{:S(2)}) %collective-permute-start) | collective-permute-done | bytes 294944 | tf_op jit(solution)/shard_map/ppermute | solution.py:97
  63.1 0.7 copy-done.9
  63.8 2.5 %terms.6 = (f32[1,384,384]{2,1,0:T(8,128)}, bf16[1,384,384]{2,1,0:T(8,128)(2,1)}) custom-call(bf16[8,768,384]{2,1,0:T(8,128)(2,1)} %convert_bitcast_fusion.half_ref, bf16[1,384,384]{2,1,0:T(8,128)(2,1)} %copy-done.9), custom_call_target="tpu_custom_call" | custom-call | tf_op jit(solution)/shard_map/terms/pallas_call | solution.py:79
  66.4 41.0 %collective-permute-done.3.comp_ref = bf16[1,384,384]{2,1,0:T(8,128)(2,1)S(1)} collective-permute-done((bf16[1,384,384]{2,1,0:T(8,128)(2,1)}, bf16[1,384,384]{2,1,0:T(8,128)(2,1)S(1)}, u32[]{:S(2)}, u32[]{:S(2)}) %collective-permute-start.3) | collective-permute-done | bytes 294944 | tf_op jit(solution)/shard_map/ppermute | solution.py:97
  107.4 0.7 copy-done.10
  108.1 2.5 %terms.7 = (f32[1,384,384]{2,1,0:T(8,128)}, bf16[1,384,384]{2,1,0:T(8,128)(2,1)}) custom-call(bf16[8,768,384]{2,1,0:T(8,128)(2,1)} %convert_bitcast_fusion.half_ref, bf16[1,384,384]{2,1,0:T(8,128)(2,1)} %copy-done.10), custom_call_target="tpu_custom_call" | custom-call | tf_op jit(solution)/shard_map/terms/pallas_call | solution.py:79
  110.6 2.7 %fusion.13.half_ref = bf16[1,768,384]{2,1,0:T(8,128)(2,1)} fusion(s32[768]{0:T(1024)S(1)} %fusion.52, bf16[8,768,384]{1,2,0:T(8,128)(2,1)} %copy-done.15), kind=kOutput, calls=%fused_computation.15 | convolution fusion | flops 453869568 | bytes 1182720 | tf_op jit(solution)/shard_map/ia,sac->sic/dot_general | solution.py:132
  113.3 5.1 %collective-permute-start.21 = (bf16[1,384,384]{2,1,0:T(8,128)(2,1)S(1)}, bf16[1,384,384]{2,1,0:T(8,128)(2,1)S(1)}, u32[]{:S(2)}, u32[]{:S(2)}) collective-permute-start(bf16[1,384,384]{2,1,0:T(8,128)(2,1)S(1)} %get-tuple-element.41), channel_id=1, source_target_pairs={{0,252},{4,248},{8,244},{12,240},{16,236},{20,232},{24,228},{28,22... | collective-permute-start | bytes 884744 | tf_op jit(solution)/shard_map/ppermute | solution.py:97
  118.4 3.1 %terms.8 = (f32[2,384,384]{2,1,0:T(8,128)}, bf16[2,384,384]{2,1,0:T(8,128)(2,1)}) custom-call(bf16[8,768,384]{2,1,0:T(8,128)(2,1)} %convert_bitcast_fusion.half_ref, bf16[2,384,384]{2,1,0:T(8,128)(2,1)} %copy-done.4), custom_call_target="tpu_custom_call" | custom-call | tf_op jit(solution)/shard_map/terms/pallas_call | solution.py:79
  121.5 0.8 copy-done.3
  122.3 3.1 %terms.9 = (f32[2,384,384]{2,1,0:T(8,128)}, bf16[2,384,384]{2,1,0:T(8,128)(2,1)}) custom-call(bf16[8,768,384]{2,1,0:T(8,128)(2,1)} %convert_bitcast_fusion.half_ref, bf16[2,384,384]{2,1,0:T(8,128)(2,1)} %copy-done.3), custom_call_target="tpu_custom_call" | custom-call | tf_op jit(solution)/shard_map/terms/pallas_call | solution.py:79
  125.5 0.7 copy-done.12
  126.2 2.5 %terms.10 = (f32[1,384,384]{2,1,0:T(8,128)}, bf16[1,384,384]{2,1,0:T(8,128)(2,1)}) custom-call(bf16[1,768,384]{2,1,0:T(8,128)(2,1)} %fusion.13.half_ref, bf16[1,384,384]{2,1,0:T(8,128)(2,1)} %copy-done.12), custom_call_target="tpu_custom_call" | custom-call | tf_op jit(solution)/shard_map/terms/pallas_call | solution.py:79
  128.8 1.5 collective-permute-start.2
  130.4 0.1 collective-permute-start.5
  130.5 8.3 %collective-permute-done.2 = bf16[1,192,384]{2,1,0:T(8,128)(2,1)S(1)} collective-permute-done((bf16[1,192,384]{2,1,0:T(8,128)(2,1)S(1)}, bf16[1,192,384]{2,1,0:T(8,128)(2,1)S(1)}, u32[]{:S(2)}, u32[]{:S(2)}) %collective-permute-start.2) | collective-permute-done | bytes 147488 | tf_op jit(solution)/shard_map/ppermute | solution.py:97
  138.8 3.1 %collective-permute-done.5 = bf16[1,192,384]{2,1,0:T(8,128)(2,1)S(1)} collective-permute-done((bf16[1,192,384]{2,1,0:T(8,128)(2,1)S(1)}, bf16[1,192,384]{2,1,0:T(8,128)(2,1)S(1)}, u32[]{:S(2)}, u32[]{:S(2)}) %collective-permute-start.5) | collective-permute-done | bytes 147488 | tf_op jit(solution)/shard_map/ppermute | solution.py:97
  142.1 0.1 collective-permute-start.8
  142.2 2.6 %collective-permute-start.7 = (bf16[2,48,384]{2,1,0:T(8,128)(2,1)S(1)}, bf16[2,48,384]{2,1,0:T(8,128)(2,1)S(1)}, u32[]{:S(2)}, u32[]{:S(2)}) collective-permute-start(bf16[2,48,384]{2,1,0:T(8,128)(2,1)S(1)} %get-tuple-element.54), channel_id=1, source_target_pairs={{0,192},{4,196},{8,200},{12,204},{16,208},{20,212},{24,216},{28,22... | collective-permute-start | bytes 221192 | tf_op jit(solution)/shard_map/ppermute | solution.py:97
  144.8 1.2 collective-permute-start.6
  146.1 0.1 collective-permute-start.10
  146.2 0.6 copy-done.11
  146.8 2.5 %terms.11 = (f32[1,384,384]{2,1,0:T(8,128)}, bf16[1,384,384]{2,1,0:T(8,128)(2,1)}) custom-call(bf16[8,768,384]{2,1,0:T(8,128)(2,1)} %convert_bitcast_fusion.half_ref, bf16[1,384,384]{2,1,0:T(8,128)(2,1)} %copy-done.11), custom_call_target="tpu_custom_call" | custom-call | tf_op jit(solution)/shard_map/terms/pallas_call | solution.py:79
  149.3 0.9 collective-permute-start.13
  150.2 0.6 collective-permute-start.22
  151.0 0.9 collective-permute-start.20
  151.9 24.8 %collective-permute-done.22 = bf16[1,384,384]{2,1,0:T(8,128)(2,1)S(1)} collective-permute-done((bf16[1,384,384]{2,1,0:T(8,128)(2,1)}, bf16[1,384,384]{2,1,0:T(8,128)(2,1)S(1)}, u32[]{:S(2)}, u32[]{:S(2)}) %collective-permute-start.22) | collective-permute-done | bytes 294944 | tf_op jit(solution)/shard_map/ppermute | solution.py:97
  176.8 0.6 collective-permute-start.23
  177.4 2.4 %collective-permute-done.20 = bf16[1,192,384]{2,1,0:T(8,128)(2,1)S(1)} collective-permute-done((bf16[1,192,384]{2,1,0:T(8,128)(2,1)S(1)}, bf16[1,192,384]{2,1,0:T(8,128)(2,1)S(1)}, u32[]{:S(2)}, u32[]{:S(2)}) %collective-permute-start.20) | collective-permute-done | bytes 147488 | tf_op jit(solution)/shard_map/ppermute | solution.py:97
  179.9 1.3 collective-permute-done.23
  181.3 0.1 convert_add_fusion.1
  181.5 0.6 collective-permute-start.11
  182.1 0.4 copy-done.1
  182.5 0.1 convert_add_fusion
  182.6 0.6 collective-permute-start.14
  183.3 0.3 collective-permute-start.26
  183.6 2.4 %collective-permute-start.25 = (bf16[2,48,384]{2,1,0:T(8,128)(2,1)S(1)}, bf16[2,48,384]{2,1,0:T(8,128)(2,1)S(1)}, u32[]{:S(2)}, u32[]{:S(2)}) collective-permute-start(bf16[2,48,384]{2,1,0:T(8,128)(2,1)S(1)} %get-tuple-element.57), channel_id=1, source_target_pairs={{0,192},{4,196},{8,200},{12,204},{16,208},{20,212},{24,216},{28,22... | collective-permute-start | bytes 221192 | tf_op jit(solution)/shard_map/ppermute | solution.py:97
  186.0 1.2 collective-permute-start.24
  187.2 1.6 collective-permute-done.11
  188.9 2.9 %collective-permute-done.14 = bf16[2,192,384]{2,1,0:T(8,128)(2,1)S(1)} collective-permute-done((bf16[2,192,384]{2,1,0:T(8,128)(2,1)S(1)}, bf16[2,192,384]{2,1,0:T(8,128)(2,1)S(1)}, u32[]{:S(2)}, u32[]{:S(2)}) %collective-permute-start.14) | collective-permute-done | bytes 294944 | tf_op jit(solution)/shard_map/ppermute | solution.py:97
  191.9 0.1 fusion.14
  192.1 0.5 collective-permute-start.17
  192.6 2.4 %collective-permute-start.16 = (bf16[4,48,384]{2,1,0:T(8,128)(2,1)S(1)}, bf16[4,48,384]{2,1,0:T(8,128)(2,1)S(1)}, u32[]{:S(2)}, u32[]{:S(2)}) collective-permute-start(bf16[4,48,384]{2,1,0:T(8,128)(2,1)S(1)} %get-tuple-element.48), channel_id=1, source_target_pairs={{0,192},{4,196},{8,200},{12,204},{16,208},{20,212},{24,216},{28,22... | collective-permute-start | bytes 442376 | tf_op jit(solution)/shard_map/ppermute | solution.py:97
  195.0 1.2 collective-permute-start.15
  196.3 3.4 %collective-permute-done.17 = bf16[4,48,384]{2,1,0:T(8,128)(2,1)S(1)} collective-permute-done((bf16[4,48,384]{2,1,0:T(8,128)(2,1)S(1)}, bf16[4,48,384]{2,1,0:T(8,128)(2,1)S(1)}, u32[]{:S(2)}, u32[]{:S(2)}) %collective-permute-start.17) | collective-permute-done | bytes 147488 | tf_op jit(solution)/shard_map/ppermute | solution.py:97
  199.7 1.3 collective-permute-done.16
  201.2 0.1 collective-permute-start.29
  201.3 4.3 %collective-permute-start.28 = (bf16[8,12,384]{2,1,0:T(8,128)(2,1)S(1)}, bf16[8,12,384]{2,1,0:T(8,128)(2,1)S(1)}, u32[]{:S(2)}, u32[]{:S(2)}) collective-permute-start(bf16[8,12,384]{2,1,0:T(8,128)(2,1)S(1)} %get-tuple-element.51), channel_id=1, source_target_pairs={{0,32},{4,36},{8,40},{12,44},{16,48},{20,52},{24,56},{28,60},{32,0... | collective-permute-start | bytes 221192 | tf_op jit(solution)/shard_map/ppermute | solution.py:97
  205.7 1.3 collective-permute-start.27
  207.0 0.2 collective-permute-done.29
  207.2 2.4 %collective-permute-done.28 = bf16[8,12,384]{2,1,0:T(8,128)(2,1)S(1)} collective-permute-done((bf16[8,12,384]{2,1,0:T(8,128)(2,1)S(1)}, bf16[8,12,384]{2,1,0:T(8,128)(2,1)S(1)}, u32[]{:S(2)}, u32[]{:S(2)}) %collective-permute-start.28) | collective-permute-done | bytes 73760 | tf_op jit(solution)/shard_map/ppermute | solution.py:97
  209.6 3.0 %collective-permute-done.27 = bf16[8,12,384]{2,1,0:T(8,128)(2,1)S(1)} collective-permute-done((bf16[8,12,384]{2,1,0:T(8,128)(2,1)S(1)}, bf16[8,12,384]{2,1,0:T(8,128)(2,1)S(1)}, u32[]{:S(2)}, u32[]{:S(2)}) %collective-permute-start.27) | collective-permute-done | bytes 73760 | tf_op jit(solution)/shard_map/ppermute | solution.py:97
  212.7 15.9 %all_gather.3 = bf16[32,12,384]{2,0,1:T(8,128)(2,1)S(1)} all-gather(bf16[8,12,384]{2,0,1:T(8,128)(2,1)S(1)} %copy.13), channel_id=1, replica_groups=mesh['pair'=64,'sec'=4] {'sec'}, dimensions={0}, use_global_device_ids=true | all-gather | bytes 368640 | tf_op jit(solution)/shard_map/all_gather | solution.py:163
  228.6 0.9 fusion.17
  (81 shorter events, 1.5 us)
Async XLA Ops:
  0.0 13.7 %copy-start = (bf16[1,8,384,384]{3,2,1,0:T(8,128)(2,1)S(1)}, bf16[1,8,384,384]{3,2,1,0:T(8,128)(2,1)}, u32[]{:S(2)}) copy-start(bf16[1,8,384,384]{3,2,1,0:T(8,128)(2,1)} %param.9) | copy-start | bytes 7077892
  0.0 25.3 %copy-start.13 = (s32[32]{0:T(128)S(1)}, s32[32]{0:T(128)}, u32[]{:S(2)}) copy-start(s32[32]{0:T(128)} %param.6) | copy-start | bytes 388
  1.9 61.2 %collective-permute-start = (bf16[1,384,384]{2,1,0:T(8,128)(2,1)}, bf16[1,384,384]{2,1,0:T(8,128)(2,1)S(1)}, u32[]{:S(2)}, u32[]{:S(2)}) collective-permute-start(bf16[1,384,384]{2,1,0:T(8,128)(2,1)} %slice_bitcast_fusion.2), channel_id=1, source_target_pairs={{0,252},{4,248},{8,244},{12,240},{16,236},{20,232},{24,228},{28,22... | collective-permute-start | bytes 884744 | tf_op jit(solution)/shard_map/ppermute | solution.py:97
  13.7 111.7 %collective-permute-start.18 = (bf16[1,384,384]{2,1,0:T(8,128)(2,1)}, bf16[1,384,384]{2,1,0:T(8,128)(2,1)S(1)}, u32[]{:S(2)}, u32[]{:S(2)}) collective-permute-start(bf16[1,384,384]{2,1,0:T(8,128)(2,1)} %get-tuple-element.42), channel_id=1, source_target_pairs={{0,252},{4,248},{8,244},{12,240},{16,236},{20,232},{24,228},{28,22... | collective-permute-start | bytes 884744 | tf_op jit(solution)/shard_map/ppermute | solution.py:97
  13.8 107.6 %collective-permute-start.12 = (bf16[2,384,384]{2,1,0:T(8,128)(2,1)S(1)}, bf16[2,384,384]{2,1,0:T(8,128)(2,1)S(1)}, u32[]{:S(2)}, u32[]{:S(2)}) collective-permute-start(bf16[2,384,384]{2,1,0:T(8,128)(2,1)S(1)} %get-tuple-element.45), channel_id=1, source_target_pairs={{0,252},{4,248},{8,244},{12,240},{16,236},{20,232},{24,228},{28,22... | collective-permute-start | bytes 1769480 | tf_op jit(solution)/shard_map/ppermute | solution.py:97
  19.6 93.7 %collective-permute-start.9 = (bf16[2,384,384]{2,1,0:T(8,128)(2,1)S(1)}, bf16[2,384,384]{2,1,0:T(8,128)(2,1)S(1)}, u32[]{:S(2)}, u32[]{:S(2)}) collective-permute-start(bf16[2,384,384]{2,1,0:T(8,128)(2,1)S(1)} %get-tuple-element.44), channel_id=1, source_target_pairs={{0,252},{4,248},{8,244},{12,240},{16,236},{20,232},{24,228},{28,22... | collective-permute-start | bytes 1769480 | tf_op jit(solution)/shard_map/ppermute | solution.py:97
  19.7 87.6 %collective-permute-start.3 = (bf16[1,384,384]{2,1,0:T(8,128)(2,1)}, bf16[1,384,384]{2,1,0:T(8,128)(2,1)S(1)}, u32[]{:S(2)}, u32[]{:S(2)}) collective-permute-start(bf16[1,384,384]{2,1,0:T(8,128)(2,1)} %get-tuple-element.43), channel_id=1, source_target_pairs={{0,252},{4,248},{8,244},{12,240},{16,236},{20,232},{24,228},{28,22... | collective-permute-start | bytes 884744 | tf_op jit(solution)/shard_map/ppermute | solution.py:97
  33.8 5.9 %copy-start.15 = (bf16[8,768,384]{1,2,0:T(8,128)(2,1)}, bf16[8,768,384]{1,2,0:T(8,128)(2,1)S(1)}, u32[]{:S(2)}) copy-start(bf16[8,768,384]{1,2,0:T(8,128)(2,1)S(1)} %convert_bitcast_fusion.1) | copy-start | bytes 14155780
  63.1 0.7 copy-start.9
  66.4 62.3 %collective-permute-start.1 = (bf16[1,384,384]{2,1,0:T(8,128)(2,1)}, bf16[1,384,384]{2,1,0:T(8,128)(2,1)S(1)}, u32[]{:S(2)}, u32[]{:S(2)}) collective-permute-start(bf16[1,384,384]{2,1,0:T(8,128)(2,1)} %get-tuple-element.24), channel_id=1, source_target_pairs={{0,64},{4,68},{8,72},{12,76},{16,80},{20,84},{24,88},{28,92},{32,9... | collective-permute-start | bytes 884744 | tf_op jit(solution)/shard_map/ppermute | solution.py:97
  107.4 0.7 copy-start.10
  110.6 19.8 %collective-permute-start.4 = (bf16[1,384,384]{2,1,0:T(8,128)(2,1)}, bf16[1,384,384]{2,1,0:T(8,128)(2,1)S(1)}, u32[]{:S(2)}, u32[]{:S(2)}) collective-permute-start(bf16[1,384,384]{2,1,0:T(8,128)(2,1)} %get-tuple-element.28), channel_id=1, source_target_pairs={{0,64},{4,68},{8,72},{12,76},{16,80},{20,84},{24,88},{28,92},{32,9... | collective-permute-start | bytes 884744 | tf_op jit(solution)/shard_map/ppermute | solution.py:97
  113.3 5.1 %copy-start.4 = (bf16[2,384,384]{2,1,0:T(8,128)(2,1)}, bf16[2,384,384]{2,1,0:T(8,128)(2,1)S(1)}, u32[]{:S(2)}) copy-start(bf16[2,384,384]{2,1,0:T(8,128)(2,1)S(1)} %collective-permute-done.9.comp_ref) | copy-start | bytes 1769476
  113.3 32.8 %collective-permute-start.21 = (bf16[1,384,384]{2,1,0:T(8,128)(2,1)S(1)}, bf16[1,384,384]{2,1,0:T(8,128)(2,1)S(1)}, u32[]{:S(2)}, u32[]{:S(2)}) collective-permute-start(bf16[1,384,384]{2,1,0:T(8,128)(2,1)S(1)} %get-tuple-element.41), channel_id=1, source_target_pairs={{0,252},{4,248},{8,244},{12,240},{16,236},{20,232},{24,228},{28,22... | collective-permute-start | bytes 884744 | tf_op jit(solution)/shard_map/ppermute | solution.py:97
  121.5 0.8 copy-start.3
  122.3 6.4 %copy-start.6 = (f32[1,384,384]{2,1,0:T(8,128)S(1)}, f32[1,384,384]{2,1,0:T(8,128)}, u32[]{:S(2)}) copy-start(f32[1,384,384]{2,1,0:T(8,128)} %get-tuple-element.23) | copy-start | bytes 1769476
  125.4 4.9 %copy-start.7 = (f32[1,384,384]{2,1,0:T(8,128)S(1)}, f32[1,384,384]{2,1,0:T(8,128)}, u32[]{:S(2)}) copy-start(f32[1,384,384]{2,1,0:T(8,128)} %get-tuple-element.27) | copy-start | bytes 1769476
  125.4 0.7 copy-start.12
  128.7 22.2 %collective-permute-start.19 = (bf16[1,384,384]{2,1,0:T(8,128)(2,1)}, bf16[1,384,384]{2,1,0:T(8,128)(2,1)S(1)}, u32[]{:S(2)}, u32[]{:S(2)}) collective-permute-start(bf16[1,384,384]{2,1,0:T(8,128)(2,1)} %get-tuple-element.37), channel_id=1, source_target_pairs={{0,8},{4,12},{8,0},{12,4},{16,24},{20,28},{24,16},{28,20},{32,40},... | collective-permute-start | bytes 884744 | tf_op jit(solution)/shard_map/ppermute | solution.py:97
  128.8 10.0 %collective-permute-start.2 = (bf16[1,192,384]{2,1,0:T(8,128)(2,1)S(1)}, bf16[1,192,384]{2,1,0:T(8,128)(2,1)S(1)}, u32[]{:S(2)}, u32[]{:S(2)}) collective-permute-start(bf16[1,192,384]{2,1,0:T(8,128)(2,1)S(1)} %slice.237), channel_id=1, source_target_pairs={{0,8},{4,12},{8,0},{12,4},{16,24},{20,28},{24,16},{28,20},{32,40},... | collective-permute-start | bytes 442376 | tf_op jit(solution)/shard_map/ppermute | solution.py:97
  130.4 11.6 %collective-permute-start.5 = (bf16[1,192,384]{2,1,0:T(8,128)(2,1)S(1)}, bf16[1,192,384]{2,1,0:T(8,128)(2,1)S(1)}, u32[]{:S(2)}, u32[]{:S(2)}) collective-permute-start(bf16[1,192,384]{2,1,0:T(8,128)(2,1)S(1)} %slice.236), channel_id=1, source_target_pairs={{0,8},{4,12},{8,0},{12,4},{16,24},{20,28},{24,16},{28,20},{32,40},... | collective-permute-start | bytes 442376 | tf_op jit(solution)/shard_map/ppermute | solution.py:97
  142.1 7.2 %collective-permute-start.8 = (bf16[2,48,384]{2,1,0:T(8,128)(2,1)S(1)}, bf16[2,48,384]{2,1,0:T(8,128)(2,1)S(1)}, u32[]{:S(2)}, u32[]{:S(2)}) collective-permute-start(bf16[2,48,384]{2,1,0:T(8,128)(2,1)S(1)} %get-tuple-element.53), channel_id=1, source_target_pairs={{0,196},{4,192},{8,204},{12,200},{16,212},{20,208},{24,220},{28,21... | collective-permute-start | bytes 221192 | tf_op jit(solution)/shard_map/ppermute | solution.py:97
  142.2 8.0 %collective-permute-start.7 = (bf16[2,48,384]{2,1,0:T(8,128)(2,1)S(1)}, bf16[2,48,384]{2,1,0:T(8,128)(2,1)S(1)}, u32[]{:S(2)}, u32[]{:S(2)}) collective-permute-start(bf16[2,48,384]{2,1,0:T(8,128)(2,1)S(1)} %get-tuple-element.54), channel_id=1, source_target_pairs={{0,192},{4,196},{8,200},{12,204},{16,208},{20,212},{24,216},{28,22... | collective-permute-start | bytes 221192 | tf_op jit(solution)/shard_map/ppermute | solution.py:97
  144.8 6.0 %collective-permute-start.6 = (bf16[2,48,384]{2,1,0:T(8,128)(2,1)S(1)}, bf16[2,48,384]{2,1,0:T(8,128)(2,1)S(1)}, u32[]{:S(2)}, u32[]{:S(2)}) collective-permute-start(bf16[2,48,384]{2,1,0:T(8,128)(2,1)S(1)} %get-tuple-element.52), channel_id=1, source_target_pairs={{0,4},{4,0},{8,12},{12,8},{16,20},{20,16},{24,28},{28,24},{32,36},... | collective-permute-start | bytes 221192 | tf_op jit(solution)/shard_map/ppermute | solution.py:97
  146.0 4.9 %copy-start.5 = (f32[1,384,384]{2,1,0:T(8,128)S(1)}, f32[1,384,384]{2,1,0:T(8,128)}, u32[]{:S(2)}) copy-start(f32[1,384,384]{2,1,0:T(8,128)} %get-tuple-element.36) | copy-start | bytes 1769476
  146.1 0.7 copy-start.11
  146.1 35.2 %collective-permute-start.10 = (bf16[2,384,384]{2,1,0:T(8,128)(2,1)}, bf16[2,384,384]{2,1,0:T(8,128)(2,1)S(1)}, u32[]{:S(2)}, u32[]{:S(2)}) collective-permute-start(bf16[2,384,384]{2,1,0:T(8,128)(2,1)} %get-tuple-element.31), channel_id=1, source_target_pairs={{0,64},{4,68},{8,72},{12,76},{16,80},{20,84},{24,88},{28,92},{32,9... | collective-permute-start | bytes 1769480 | tf_op jit(solution)/shard_map/ppermute | solution.py:97
  149.3 27.4 %copy-start.8 = (f32[1,384,384]{2,1,0:T(8,128)S(1)}, f32[1,384,384]{2,1,0:T(8,128)}, u32[]{:S(2)}) copy-start(f32[1,384,384]{2,1,0:T(8,128)} %get-tuple-element.39) | copy-start | bytes 1769476
  149.3 32.8 %collective-permute-start.13 = (bf16[2,384,384]{2,1,0:T(8,128)(2,1)}, bf16[2,384,384]{2,1,0:T(8,128)(2,1)S(1)}, u32[]{:S(2)}, u32[]{:S(2)}) collective-permute-start(bf16[2,384,384]{2,1,0:T(8,128)(2,1)} %get-tuple-element.34), channel_id=1, source_target_pairs={{0,64},{4,68},{8,72},{12,76},{16,80},{20,84},{24,88},{28,92},{32,9... | collective-permute-start | bytes 1769480 | tf_op jit(solution)/shard_map/ppermute | solution.py:97
  150.2 26.5 %collective-permute-start.22 = (bf16[1,384,384]{2,1,0:T(8,128)(2,1)}, bf16[1,384,384]{2,1,0:T(8,128)(2,1)S(1)}, u32[]{:S(2)}, u32[]{:S(2)}) collective-permute-start(bf16[1,384,384]{2,1,0:T(8,128)(2,1)} %get-tuple-element.40), channel_id=1, source_target_pairs={{0,64},{4,68},{8,72},{12,76},{16,80},{20,84},{24,88},{28,92},{32,9... | collective-permute-start | bytes 884744 | tf_op jit(solution)/shard_map/ppermute | solution.py:97
  151.0 30.3 %copy-start.2 = (f32[2,384,384]{2,1,0:T(8,128)S(1)}, f32[2,384,384]{2,1,0:T(8,128)}, u32[]{:S(2)}) copy-start(f32[2,384,384]{2,1,0:T(8,128)} %get-tuple-element.30) | copy-start | bytes 3538948
  151.0 28.9 %collective-permute-start.20 = (bf16[1,192,384]{2,1,0:T(8,128)(2,1)S(1)}, bf16[1,192,384]{2,1,0:T(8,128)(2,1)S(1)}, u32[]{:S(2)}, u32[]{:S(2)}) collective-permute-start(bf16[1,192,384]{2,1,0:T(8,128)(2,1)S(1)} %slice.235), channel_id=1, source_target_pairs={{0,64},{4,68},{8,72},{12,76},{16,80},{20,84},{24,88},{28,92},{32,9... | collective-permute-start | bytes 442376 | tf_op jit(solution)/shard_map/ppermute | solution.py:97
  176.8 4.4 %collective-permute-start.23 = (bf16[1,192,384]{2,1,0:T(8,128)(2,1)S(1)}, bf16[1,192,384]{2,1,0:T(8,128)(2,1)S(1)}, u32[]{:S(2)}, u32[]{:S(2)}) collective-permute-start(bf16[1,192,384]{2,1,0:T(8,128)(2,1)S(1)} %slice.234), channel_id=1, source_target_pairs={{0,8},{4,12},{8,0},{12,4},{16,24},{20,28},{24,16},{28,20},{32,40},... | collective-permute-start | bytes 442376 | tf_op jit(solution)/shard_map/ppermute | solution.py:97
  181.2 1.3 copy-start.1
  181.5 7.4 %collective-permute-start.11 = (bf16[2,192,384]{2,1,0:T(8,128)(2,1)S(1)}, bf16[2,192,384]{2,1,0:T(8,128)(2,1)S(1)}, u32[]{:S(2)}, u32[]{:S(2)}) collective-permute-start(bf16[2,192,384]{2,1,0:T(8,128)(2,1)S(1)} %slice.233), channel_id=1, source_target_pairs={{0,8},{4,12},{8,0},{12,4},{16,24},{20,28},{24,16},{28,20},{32,40},... | collective-permute-start | bytes 884744 | tf_op jit(solution)/shard_map/ppermute | solution.py:97
  182.6 9.2 %collective-permute-start.14 = (bf16[2,192,384]{2,1,0:T(8,128)(2,1)S(1)}, bf16[2,192,384]{2,1,0:T(8,128)(2,1)S(1)}, u32[]{:S(2)}, u32[]{:S(2)}) collective-permute-start(bf16[2,192,384]{2,1,0:T(8,128)(2,1)S(1)} %slice.232), channel_id=1, source_target_pairs={{0,8},{4,12},{8,0},{12,4},{16,24},{20,28},{24,16},{28,20},{32,40},... | collective-permute-start | bytes 884744 | tf_op jit(solution)/shard_map/ppermute | solution.py:97
  183.3 11.7 %collective-permute-start.26 = (bf16[2,48,384]{2,1,0:T(8,128)(2,1)S(1)}, bf16[2,48,384]{2,1,0:T(8,128)(2,1)S(1)}, u32[]{:S(2)}, u32[]{:S(2)}) collective-permute-start(bf16[2,48,384]{2,1,0:T(8,128)(2,1)S(1)} %get-tuple-element.56), channel_id=1, source_target_pairs={{0,196},{4,192},{8,204},{12,200},{16,212},{20,208},{24,220},{28,21... | collective-permute-start | bytes 221192 | tf_op jit(solution)/shard_map/ppermute | solution.py:97
  183.6 12.7 %collective-permute-start.25 = (bf16[2,48,384]{2,1,0:T(8,128)(2,1)S(1)}, bf16[2,48,384]{2,1,0:T(8,128)(2,1)S(1)}, u32[]{:S(2)}, u32[]{:S(2)}) collective-permute-start(bf16[2,48,384]{2,1,0:T(8,128)(2,1)S(1)} %get-tuple-element.57), channel_id=1, source_target_pairs={{0,192},{4,196},{8,200},{12,204},{16,208},{20,212},{24,216},{28,22... | collective-permute-start | bytes 221192 | tf_op jit(solution)/shard_map/ppermute | solution.py:97
  186.0 10.2 %collective-permute-start.24 = (bf16[2,48,384]{2,1,0:T(8,128)(2,1)S(1)}, bf16[2,48,384]{2,1,0:T(8,128)(2,1)S(1)}, u32[]{:S(2)}, u32[]{:S(2)}) collective-permute-start(bf16[2,48,384]{2,1,0:T(8,128)(2,1)S(1)} %get-tuple-element.55), channel_id=1, source_target_pairs={{0,4},{4,0},{8,12},{12,8},{16,20},{20,16},{24,28},{28,24},{32,36},... | collective-permute-start | bytes 221192 | tf_op jit(solution)/shard_map/ppermute | solution.py:97
  192.1 7.7 %collective-permute-start.17 = (bf16[4,48,384]{2,1,0:T(8,128)(2,1)S(1)}, bf16[4,48,384]{2,1,0:T(8,128)(2,1)S(1)}, u32[]{:S(2)}, u32[]{:S(2)}) collective-permute-start(bf16[4,48,384]{2,1,0:T(8,128)(2,1)S(1)} %get-tuple-element.47), channel_id=1, source_target_pairs={{0,196},{4,192},{8,204},{12,200},{16,212},{20,208},{24,220},{28,21... | collective-permute-start | bytes 442376 | tf_op jit(solution)/shard_map/ppermute | solution.py:97
  192.6 8.4 %collective-permute-start.16 = (bf16[4,48,384]{2,1,0:T(8,128)(2,1)S(1)}, bf16[4,48,384]{2,1,0:T(8,128)(2,1)S(1)}, u32[]{:S(2)}, u32[]{:S(2)}) collective-permute-start(bf16[4,48,384]{2,1,0:T(8,128)(2,1)S(1)} %get-tuple-element.48), channel_id=1, source_target_pairs={{0,192},{4,196},{8,200},{12,204},{16,208},{20,212},{24,216},{28,22... | collective-permute-start | bytes 442376 | tf_op jit(solution)/shard_map/ppermute | solution.py:97
  195.0 6.0 %collective-permute-start.15 = (bf16[4,48,384]{2,1,0:T(8,128)(2,1)S(1)}, bf16[4,48,384]{2,1,0:T(8,128)(2,1)S(1)}, u32[]{:S(2)}, u32[]{:S(2)}) collective-permute-start(bf16[4,48,384]{2,1,0:T(8,128)(2,1)S(1)} %get-tuple-element.46), channel_id=1, source_target_pairs={{0,4},{4,0},{8,12},{12,8},{16,20},{20,16},{24,28},{28,24},{32,36},... | collective-permute-start | bytes 442376 | tf_op jit(solution)/shard_map/ppermute | solution.py:97
  201.1 27.5 %copy-start.14 = (s32[32]{0:T(128)S(1)}, s32[32]{0:T(128)}, u32[]{:S(2)}) copy-start(s32[32]{0:T(128)} %param.7) | copy-start | bytes 388
  201.2 6.0 %collective-permute-start.29 = (bf16[8,12,384]{2,1,0:T(8,128)(2,1)S(1)}, bf16[8,12,384]{2,1,0:T(8,128)(2,1)S(1)}, u32[]{:S(2)}, u32[]{:S(2)}) collective-permute-start(bf16[8,12,384]{2,1,0:T(8,128)(2,1)S(1)} %get-tuple-element.50), channel_id=1, source_target_pairs={{0,48},{4,52},{8,56},{12,60},{16,32},{20,36},{24,40},{28,44},{32,1... | collective-permute-start | bytes 221192 | tf_op jit(solution)/shard_map/ppermute | solution.py:97
  201.3 8.3 %collective-permute-start.28 = (bf16[8,12,384]{2,1,0:T(8,128)(2,1)S(1)}, bf16[8,12,384]{2,1,0:T(8,128)(2,1)S(1)}, u32[]{:S(2)}, u32[]{:S(2)}) collective-permute-start(bf16[8,12,384]{2,1,0:T(8,128)(2,1)S(1)} %get-tuple-element.51), channel_id=1, source_target_pairs={{0,32},{4,36},{8,40},{12,44},{16,48},{20,52},{24,56},{28,60},{32,0... | collective-permute-start | bytes 221192 | tf_op jit(solution)/shard_map/ppermute | solution.py:97
  205.7 6.9 %collective-permute-start.27 = (bf16[8,12,384]{2,1,0:T(8,128)(2,1)S(1)}, bf16[8,12,384]{2,1,0:T(8,128)(2,1)S(1)}, u32[]{:S(2)}, u32[]{:S(2)}) collective-permute-start(bf16[8,12,384]{2,1,0:T(8,128)(2,1)S(1)} %get-tuple-element.49), channel_id=1, source_target_pairs={{0,16},{4,20},{8,24},{12,28},{16,0},{20,4},{24,8},{28,12},{32,48},... | collective-permute-start | bytes 221192 | tf_op jit(solution)/shard_map/ppermute | solution.py:97
